TPU v7x, 512 devices: a whole 4x8x8 slice. The times are simulated.
512 devices in a mesh: sta: 64 (over y, z_hi, x), stk: 8 (over z_lo, core).
Axes of the slice: x: 4, y: 8, z: 8 (z_hi: 2, z_lo: 4; z = z_hi * 4 + z_lo), core: 2. Of those that a mesh axis runs over, the one named last changes fastest.
Arguments:
- spectra: float32 [8, 256, 2, 2048], P('stk', 'sta')
- partner_masks: int32 [4], replicated, may hold values from 1 to 63, as said below
Outputs:
- correlations: float32 [1024, 4, 2400], P(('sta', 'stk'))
Inputs may be any that keep to these rules, and one draw needn't show every extreme that they name: `partner_masks`: each round's block pairing is b with b XOR mask; every bit below log2 of the number of station blocks is set in some round's mask.
All inputs are finite; a program needn't handle non-finite values.
Results may differ from a plain program's by a relative error of at most 0.0037.
Values may be sent and summed in bfloat16 or wider, within the bound.
No kernel may reach another device: no remote copies, remote signals or barrier semaphores. Data moves between devices by JAX's collectives and lax.ppermute only.
A program may use at most 64 MiB of HBM per device.

v0:
```python
import math

import jax
import jax.numpy as jnp
from jax import lax
from jax.sharding import PartitionSpec as P

NFFT = 8192
MAXLAG = 1200


def from_partner(array, axis, bit):
    return lax.ppermute(array, axis, [(i, i ^ 1 << bit) for i in range(lax.axis_size(axis))])


def follow_mask(block_data, round_mask):
    current = block_data
    for bit_index in range(lax.axis_size("sta").bit_length() - 1):
        swapped = from_partner(current, "sta", bit_index)
        flag_set = jnp.bitwise_and(jnp.right_shift(round_mask, bit_index), 1) == 1
        current = jnp.where(flag_set, swapped, current)
    return current


def cross_spectrum(own_block, partner_block):
    own_float = own_block.astype(jnp.float32)
    far_float = partner_block.astype(jnp.float32)
    own_re = own_float[:, :, 0]
    own_im = own_float[:, :, 1]
    far_re = far_float[:, :, 0]
    far_im = far_float[:, :, 1]
    real_part = jnp.einsum("wik,wjk->ijk", own_re, far_re) + jnp.einsum(
        "wik,wjk->ijk", own_im, far_im
    )
    imag_part = jnp.einsum("wik,wjk->ijk", own_im, far_re) - jnp.einsum(
        "wik,wjk->ijk", own_re, far_im
    )
    joined = jnp.stack([real_part, imag_part], axis=2)
    return joined.reshape(joined.shape[0] * joined.shape[1], 2, joined.shape[3])


def angle_table(first_index, second_index, period):
    product = jnp.remainder(first_index[:, None] * second_index[None, :], period).astype(
        jnp.float32
    )
    angle = product * jnp.float32(2.0 * math.pi / period)
    return (jnp.cos(angle), jnp.sin(angle))


def transform(spec_rows):
    row_count, _, bin_count = spec_rows.shape
    fine_width = 128
    coarse_period = NFFT // fine_width
    outer_count = bin_count // coarse_period
    group_count = (2 * MAXLAG + fine_width - 1) // fine_width
    highest = lax.Precision.HIGHEST
    bin_index = jnp.arange(bin_count, dtype=jnp.int32)
    shift_angle = jnp.remainder(bin_index * (NFFT - MAXLAG), NFFT).astype(
        jnp.float32
    ) * jnp.float32(2.0 * math.pi / NFFT)
    bin_weight = jnp.where(bin_index == 0, 1.0, 2.0).astype(jnp.float32)
    shift_cos = bin_weight * jnp.cos(shift_angle)
    shift_sin = bin_weight * jnp.sin(shift_angle)
    spec_re = spec_rows[:, 0]
    spec_im = spec_rows[:, 1]
    rotated_re = (spec_re * shift_cos - spec_im * shift_sin).reshape(
        row_count, outer_count, coarse_period
    )
    rotated_im = (spec_re * shift_sin + spec_im * shift_cos).reshape(
        row_count, outer_count, coarse_period
    )
    outer_index = jnp.arange(outer_count, dtype=jnp.int32)
    fine_index = jnp.arange(fine_width, dtype=jnp.int32)
    coarse_index = jnp.arange(coarse_period, dtype=jnp.int32)
    group_index = jnp.arange(group_count, dtype=jnp.int32)
    first_cos, first_sin = angle_table(outer_index, fine_index, fine_width)
    inner_re = jnp.einsum("rac,af->rcf", rotated_re, first_cos, precision=highest) - jnp.einsum(
        "rac,af->rcf", rotated_im, first_sin, precision=highest
    )
    inner_im = jnp.einsum("rac,af->rcf", rotated_re, first_sin, precision=highest) + jnp.einsum(
        "rac,af->rcf", rotated_im, first_cos, precision=highest
    )
    twist_cos, twist_sin = angle_table(coarse_index, fine_index, NFFT)
    turned_re = inner_re * twist_cos - inner_im * twist_sin
    turned_im = inner_re * twist_sin + inner_im * twist_cos
    last_cos, last_sin = angle_table(coarse_index, group_index, coarse_period)
    series = jnp.einsum("rcf,cg->rgf", turned_re, last_cos, precision=highest) - jnp.einsum(
        "rcf,cg->rgf", turned_im, last_sin, precision=highest
    )
    return series.reshape(row_count, group_count * fine_width)[:, : 2 * MAXLAG]


def body(spectra, partner_masks):
    windows_here, block_size, _, bin_count = spectra.shape
    power_spec = spectra[:, :, 0] ** 2 + spectra[:, :, 1] ** 2
    water_base = jnp.mean(power_spec, axis=-1, keepdims=True)
    denom = jnp.sqrt(power_spec + 0.05 * (water_base + 1e-06))
    whitened = (spectra / denom[:, :, None, :]).astype(jnp.bfloat16)
    round_total = partner_masks.shape[0]
    cross_list = []
    for round_index in range(round_total):
        round_mask = partner_masks[round_index]
        partner_block = follow_mask(whitened, round_mask)
        cross_list.append(cross_spectrum(whitened, partner_block))
    cross_spec = jnp.stack(cross_list, axis=1)
    normalizer = 1.0 / math.sqrt(windows_here * lax.axis_size("stk") * bin_count)
    row_count = cross_spec.shape[0] // lax.axis_size("stk") * lax.axis_size("stk")
    lagged_rows = transform(cross_spec.reshape(row_count * round_total, 2, bin_count))
    correlations = lax.psum_scatter(
        lagged_rows.reshape(row_count, round_total, 2 * MAXLAG),
        "stk",
        scatter_dimension=0,
        tiled=True,
    )
    return correlations * normalizer


def solution(mesh):
    return jax.shard_map(
        body,
        mesh=mesh,
        in_specs=(P("stk", "sta", None, None), P()),
        out_specs=P(("sta", "stk"), None, None),
        check_vma=False,
    )
```

profile of v0, /device:TPU:1, one launch (start us, length us, event | category | flops | bytes accessed | tf_op | source)
XLA Modules:
  0.0 224.9 jit_solution(15368133924588336178)
XLA Ops:
  8.7 3.9 %collective-permute-start = (bf16[1,4,2,2048]{3,2,1,0:T(2,128)(2,1)S(1)}, bf16[1,4,2,2048]{3,2,1,0:T(2,128)(2,1)S(1)}, u32[]{:S(2)}, u32[]{:S(2)}) collective-permute-start(bf16[1,4,2,2048]{3,2,1,0:T(2,128)(2,1)S(1)} %divide_convert_fusion), channel_id=1, source_target_pairs={{0,8},{8,0},{16,24},{24,16},{32,40},{40,32},{48,56},{56,48},{64,72... | collective-permute-start | bytes 98312 | tf_op jit(solution)/shard_map/ppermute | solution.py:13
  12.9 1.5 fusion.83
  17.9 4.4 %collective-permute-start.16 = (bf16[1,4,2,2048]{3,2,1,0:T(2,128)(2,1)S(1)}, bf16[1,4,2,2048]{3,2,1,0:T(2,128)(2,1)S(1)}, u32[]{:S(2)}, u32[]{:S(2)}) collective-permute-start(bf16[1,4,2,2048]{3,2,1,0:T(2,128)(2,1)S(1)} %get-tuple-element.24), channel_id=1, source_target_pairs={{0,16},{8,24},{16,0},{24,8},{32,48},{40,56},{48,32},{56,40},{64,80... | collective-permute-start | bytes 98312 | tf_op jit(solution)/shard_map/ppermute | solution.py:13
  35.1 2.4 %collective-permute-start.11 = (bf16[1,4,2,2048]{3,2,1,0:T(2,128)(2,1)S(1)}, bf16[1,4,2,2048]{3,2,1,0:T(2,128)(2,1)S(1)}, u32[]{:S(2)}, u32[]{:S(2)}) collective-permute-start(bf16[1,4,2,2048]{3,2,1,0:T(2,128)(2,1)S(1)} %get-tuple-element.25), channel_id=1, source_target_pairs={{0,16},{8,24},{16,0},{24,8},{32,48},{40,56},{48,32},{56,40},{64,80... | collective-permute-start | bytes 98312 | tf_op jit(solution)/shard_map/ppermute | solution.py:13
  37.5 4.4 %collective-permute-start.6 = (bf16[1,4,2,2048]{3,2,1,0:T(2,128)(2,1)S(1)}, bf16[1,4,2,2048]{3,2,1,0:T(2,128)(2,1)S(1)}, u32[]{:S(2)}, u32[]{:S(2)}) collective-permute-start(bf16[1,4,2,2048]{3,2,1,0:T(2,128)(2,1)S(1)} %get-tuple-element.26), channel_id=1, source_target_pairs={{0,16},{8,24},{16,0},{24,8},{32,48},{40,56},{48,32},{56,40},{64,80... | collective-permute-start | bytes 98312 | tf_op jit(solution)/shard_map/ppermute | solution.py:13
  41.9 2.4 %collective-permute-start.1 = (bf16[1,4,2,2048]{3,2,1,0:T(2,128)(2,1)S(1)}, bf16[1,4,2,2048]{3,2,1,0:T(2,128)(2,1)S(1)}, u32[]{:S(2)}, u32[]{:S(2)}) collective-permute-start(bf16[1,4,2,2048]{3,2,1,0:T(2,128)(2,1)S(1)} %get-tuple-element.23), channel_id=1, source_target_pairs={{0,16},{8,24},{16,0},{24,8},{32,48},{40,56},{48,32},{56,40},{64,80... | collective-permute-start | bytes 98312 | tf_op jit(solution)/shard_map/ppermute | solution.py:13
  44.4 10.6 %collective-permute-start.17 = (bf16[1,4,2,2048]{3,2,1,0:T(2,128)(2,1)S(1)}, bf16[1,4,2,2048]{3,2,1,0:T(2,128)(2,1)S(1)}, u32[]{:S(2)}, u32[]{:S(2)}) collective-permute-start(bf16[1,4,2,2048]{3,2,1,0:T(2,128)(2,1)S(1)} %bitcast.180), channel_id=1, source_target_pairs={{0,32},{8,40},{16,48},{24,56},{32,0},{40,8},{48,16},{56,24},{64,96... | collective-permute-start | bytes 98312 | tf_op jit(solution)/shard_map/ppermute | solution.py:13
  55.0 1.9 collective-permute-start.12
  57.0 7.3 %collective-permute-start.7 = (bf16[1,4,2,2048]{3,2,1,0:T(2,128)(2,1)S(1)}, bf16[1,4,2,2048]{3,2,1,0:T(2,128)(2,1)S(1)}, u32[]{:S(2)}, u32[]{:S(2)}) collective-permute-start(bf16[1,4,2,2048]{3,2,1,0:T(2,128)(2,1)S(1)} %bitcast.182), channel_id=1, source_target_pairs={{0,32},{8,40},{16,48},{24,56},{32,0},{40,8},{48,16},{56,24},{64,96... | collective-permute-start | bytes 98312 | tf_op jit(solution)/shard_map/ppermute | solution.py:13
  64.3 1.9 collective-permute-start.2
  66.3 3.2 %collective-permute-start.18 = (bf16[1,4,2,2048]{3,2,1,0:T(2,128)(2,1)S(1)}, bf16[1,4,2,2048]{3,2,1,0:T(2,128)(2,1)S(1)}, u32[]{:S(2)}, u32[]{:S(2)}) collective-permute-start(bf16[1,4,2,2048]{3,2,1,0:T(2,128)(2,1)S(1)} %bitcast.184), channel_id=1, source_target_pairs={{0,64},{8,72},{16,80},{24,88},{32,96},{40,104},{48,112},{56,120},{... | collective-permute-start | bytes 98312 | tf_op jit(solution)/shard_map/ppermute | solution.py:13
  69.5 2.1 collective-permute-start.13
  71.6 3.2 %collective-permute-start.8 = (bf16[1,4,2,2048]{3,2,1,0:T(2,128)(2,1)S(1)}, bf16[1,4,2,2048]{3,2,1,0:T(2,128)(2,1)S(1)}, u32[]{:S(2)}, u32[]{:S(2)}) collective-permute-start(bf16[1,4,2,2048]{3,2,1,0:T(2,128)(2,1)S(1)} %bitcast.186), channel_id=1, source_target_pairs={{0,64},{8,72},{16,80},{24,88},{32,96},{40,104},{48,112},{56,120},{... | collective-permute-start | bytes 98312 | tf_op jit(solution)/shard_map/ppermute | solution.py:13
  74.9 2.1 collective-permute-start.3
  77.0 4.2 %collective-permute-start.19 = (bf16[1,4,2,2048]{3,2,1,0:T(2,128)(2,1)S(1)}, bf16[1,4,2,2048]{3,2,1,0:T(2,128)(2,1)S(1)}, u32[]{:S(2)}, u32[]{:S(2)}) collective-permute-start(bf16[1,4,2,2048]{3,2,1,0:T(2,128)(2,1)S(1)} %bitcast.188), channel_id=1, source_target_pairs={{0,128},{8,136},{16,144},{24,152},{32,160},{40,168},{48,176},{56,1... | collective-permute-start | bytes 98312 | tf_op jit(solution)/shard_map/ppermute | solution.py:13
  81.2 2.0 collective-permute-start.14
  83.2 4.2 %collective-permute-start.9 = (bf16[1,4,2,2048]{3,2,1,0:T(2,128)(2,1)S(1)}, bf16[1,4,2,2048]{3,2,1,0:T(2,128)(2,1)S(1)}, u32[]{:S(2)}, u32[]{:S(2)}) collective-permute-start(bf16[1,4,2,2048]{3,2,1,0:T(2,128)(2,1)S(1)} %bitcast.190), channel_id=1, source_target_pairs={{0,128},{8,136},{16,144},{24,152},{32,160},{40,168},{48,176},{56,1... | collective-permute-start | bytes 98312 | tf_op jit(solution)/shard_map/ppermute | solution.py:13
  87.5 2.0 collective-permute-start.4
  89.5 7.5 %collective-permute-start.20 = (bf16[1,4,2,2048]{3,2,1,0:T(2,128)(2,1)S(1)}, bf16[1,4,2,2048]{3,2,1,0:T(2,128)(2,1)S(1)}, u32[]{:S(2)}, u32[]{:S(2)}) collective-permute-start(bf16[1,4,2,2048]{3,2,1,0:T(2,128)(2,1)S(1)} %bitcast.192), channel_id=1, source_target_pairs={{0,256},{8,264},{16,272},{24,280},{32,288},{40,296},{48,304},{56,3... | collective-permute-start | bytes 98312 | tf_op jit(solution)/shard_map/ppermute | solution.py:13
  97.0 1.9 collective-permute-start.15
  98.9 7.3 %collective-permute-start.10 = (bf16[1,4,2,2048]{3,2,1,0:T(2,128)(2,1)S(1)}, bf16[1,4,2,2048]{3,2,1,0:T(2,128)(2,1)S(1)}, u32[]{:S(2)}, u32[]{:S(2)}) collective-permute-start(bf16[1,4,2,2048]{3,2,1,0:T(2,128)(2,1)S(1)} %bitcast.194), channel_id=1, source_target_pairs={{0,256},{8,264},{16,272},{24,280},{32,288},{40,296},{48,304},{56,3... | collective-permute-start | bytes 98312 | tf_op jit(solution)/shard_map/ppermute | solution.py:13
  106.2 2.1 collective-permute-start.5
  108.6 6.5 %collective-permute-done.5 = bf16[1,4,2,2048]{3,2,1,0:T(2,128)(2,1)S(1)} collective-permute-done((bf16[1,4,2,2048]{3,2,1,0:T(2,128)(2,1)S(1)}, bf16[1,4,2,2048]{3,2,1,0:T(2,128)(2,1)S(1)}, u32[]{:S(2)}, u32[]{:S(2)}) %collective-permute-start.5) | collective-permute-done | bytes 32800 | tf_op jit(solution)/shard_map/ppermute | solution.py:13
  119.3 3.5 %fusion.16 = f32[64,64,128]{2,1,0:T(8,128)S(1)} fusion(f32[64,32,64]{2,1,0:T(8,128)S(1)} %squeeze.5, f32[64,32,64]{2,1,0:T(8,128)S(1)} %squeeze.4, f32[32,64]{1,0:T(8,128)S(1)} %get-tuple-element.51, f32[32,64]{1,0:T(8,128)S(1)} %get-tuple-element.52), kind=kOutput, calls=%fused_computation.20 | convolution fusion | flops 201777152 | bytes 3162112 | tf_op jit(solution)/shard_map/rac,af->rcf/dot_general | solution.py:77
  122.8 3.5 %fusion.15 = f32[64,64,128]{2,1,0:T(8,128)S(1)} fusion(f32[64,32,64]{2,1,0:T(8,128)S(1)} %squeeze.5, f32[64,32,64]{2,1,0:T(8,128)S(1)} %squeeze.4, f32[32,64]{1,0:T(8,128)S(1)} %get-tuple-element.51, f32[32,64]{1,0:T(8,128)S(1)} %get-tuple-element.52), kind=kOutput, calls=%fused_computation.19 | convolution fusion | flops 201777152 | bytes 3162112 | tf_op jit(solution)/shard_map/rac,af->rcf/dot_general | solution.py:80
  126.3 3.7 %convolution_subtract_fusion = f32[64,64,128]{2,1,0:T(8,128)S(1)} fusion(f32[64,64,128]{2,1,0:T(8,128)S(1)} %fusion.16, f32[64,32,64]{2,1,0:T(8,128)S(1)} %squeeze.5, f32[64,32,64]{2,1,0:T(8,128)S(1)} %squeeze.4, f32[32,64]{1,0:T(8,128)S(1)} %get-tuple-element.51, f32[32,64]{1,0:T(8,128)S(1)} %get-tuple-element.52), kind=kOutput, calls=%fused_computation.9 | convolution fusion | flops 202301440 | bytes 5259264 | tf_op jit(solution)/shard_map/rac,af->rcf/dot_general | solution.py:77
  130.0 3.5 %convolution_add_fusion = f32[64,64,128]{2,1,0:T(8,128)S(1)} fusion(f32[64,64,128]{2,1,0:T(8,128)S(1)} %fusion.15, f32[64,32,64]{2,1,0:T(8,128)S(1)} %squeeze.5, f32[64,32,64]{2,1,0:T(8,128)S(1)} %squeeze.4, f32[32,64]{1,0:T(8,128)S(1)} %get-tuple-element.51, f32[32,64]{1,0:T(8,128)S(1)} %get-tuple-element.52), kind=kOutput, calls=%fused_computation.8 | convolution fusion | flops 202301440 | bytes 5259264 | tf_op jit(solution)/shard_map/rac,af->rcf/dot_general | solution.py:80
  133.5 1.4 fusion
  134.9 1.4 fusion.8
  137.5 1.3 dynamic-slice
  139.4 77.0 %all-reduce.3.cloned.1.call-done = f32[16,4,2400]{2,1,0:T(4,128)} async-done(((f32[16,4,2400]{2,1,0:T(4,128)}), f32[16,4,2400]{2,1,0:T(4,128)}) %all-reduce.3.cloned.1.call-update) | async-done | bytes 614416
  216.5 1.5 dynamic-slice_multiply_fusion
  (76 shorter events, 9.0 us)
Async XLA Ops:
  6.5 209.9 %all-reduce.3.cloned.1.call-start = ((), (), s32[]{:S(2)}) async-start(), calls=%async_computation | async-start | bytes 1245184
  8.7 8.2 %collective-permute-start = (bf16[1,4,2,2048]{3,2,1,0:T(2,128)(2,1)S(1)}, bf16[1,4,2,2048]{3,2,1,0:T(2,128)(2,1)S(1)}, u32[]{:S(2)}, u32[]{:S(2)}) collective-permute-start(bf16[1,4,2,2048]{3,2,1,0:T(2,128)(2,1)S(1)} %divide_convert_fusion), channel_id=1, source_target_pairs={{0,8},{8,0},{16,24},{24,16},{32,40},{40,32},{48,56},{56,48},{64,72... | collective-permute-start | bytes 98312 | tf_op jit(solution)/shard_map/ppermute | solution.py:13
  17.9 26.5 %collective-permute-start.16 = (bf16[1,4,2,2048]{3,2,1,0:T(2,128)(2,1)S(1)}, bf16[1,4,2,2048]{3,2,1,0:T(2,128)(2,1)S(1)}, u32[]{:S(2)}, u32[]{:S(2)}) collective-permute-start(bf16[1,4,2,2048]{3,2,1,0:T(2,128)(2,1)S(1)} %get-tuple-element.24), channel_id=1, source_target_pairs={{0,16},{8,24},{16,0},{24,8},{32,48},{40,56},{48,32},{56,40},{64,80... | collective-permute-start | bytes 98312 | tf_op jit(solution)/shard_map/ppermute | solution.py:13
  35.1 19.9 %collective-permute-start.11 = (bf16[1,4,2,2048]{3,2,1,0:T(2,128)(2,1)S(1)}, bf16[1,4,2,2048]{3,2,1,0:T(2,128)(2,1)S(1)}, u32[]{:S(2)}, u32[]{:S(2)}) collective-permute-start(bf16[1,4,2,2048]{3,2,1,0:T(2,128)(2,1)S(1)} %get-tuple-element.25), channel_id=1, source_target_pairs={{0,16},{8,24},{16,0},{24,8},{32,48},{40,56},{48,32},{56,40},{64,80... | collective-permute-start | bytes 98312 | tf_op jit(solution)/shard_map/ppermute | solution.py:13
  37.5 19.4 %collective-permute-start.6 = (bf16[1,4,2,2048]{3,2,1,0:T(2,128)(2,1)S(1)}, bf16[1,4,2,2048]{3,2,1,0:T(2,128)(2,1)S(1)}, u32[]{:S(2)}, u32[]{:S(2)}) collective-permute-start(bf16[1,4,2,2048]{3,2,1,0:T(2,128)(2,1)S(1)} %get-tuple-element.26), channel_id=1, source_target_pairs={{0,16},{8,24},{16,0},{24,8},{32,48},{40,56},{48,32},{56,40},{64,80... | collective-permute-start | bytes 98312 | tf_op jit(solution)/shard_map/ppermute | solution.py:13
  41.9 22.4 %collective-permute-start.1 = (bf16[1,4,2,2048]{3,2,1,0:T(2,128)(2,1)S(1)}, bf16[1,4,2,2048]{3,2,1,0:T(2,128)(2,1)S(1)}, u32[]{:S(2)}, u32[]{:S(2)}) collective-permute-start(bf16[1,4,2,2048]{3,2,1,0:T(2,128)(2,1)S(1)} %get-tuple-element.23), channel_id=1, source_target_pairs={{0,16},{8,24},{16,0},{24,8},{32,48},{40,56},{48,32},{56,40},{64,80... | collective-permute-start | bytes 98312 | tf_op jit(solution)/shard_map/ppermute | solution.py:13
  44.4 21.9 %collective-permute-start.17 = (bf16[1,4,2,2048]{3,2,1,0:T(2,128)(2,1)S(1)}, bf16[1,4,2,2048]{3,2,1,0:T(2,128)(2,1)S(1)}, u32[]{:S(2)}, u32[]{:S(2)}) collective-permute-start(bf16[1,4,2,2048]{3,2,1,0:T(2,128)(2,1)S(1)} %bitcast.180), channel_id=1, source_target_pairs={{0,32},{8,40},{16,48},{24,56},{32,0},{40,8},{48,16},{56,24},{64,96... | collective-permute-start | bytes 98312 | tf_op jit(solution)/shard_map/ppermute | solution.py:13
  55.0 14.4 %collective-permute-start.12 = (bf16[1,4,2,2048]{3,2,1,0:T(2,128)(2,1)S(1)}, bf16[1,4,2,2048]{3,2,1,0:T(2,128)(2,1)S(1)}, u32[]{:S(2)}, u32[]{:S(2)}) collective-permute-start(bf16[1,4,2,2048]{3,2,1,0:T(2,128)(2,1)S(1)} %bitcast.181), channel_id=1, source_target_pairs={{0,32},{8,40},{16,48},{24,56},{32,0},{40,8},{48,16},{56,24},{64,96... | collective-permute-start | bytes 98312 | tf_op jit(solution)/shard_map/ppermute | solution.py:13
  57.0 14.6 %collective-permute-start.7 = (bf16[1,4,2,2048]{3,2,1,0:T(2,128)(2,1)S(1)}, bf16[1,4,2,2048]{3,2,1,0:T(2,128)(2,1)S(1)}, u32[]{:S(2)}, u32[]{:S(2)}) collective-permute-start(bf16[1,4,2,2048]{3,2,1,0:T(2,128)(2,1)S(1)} %bitcast.182), channel_id=1, source_target_pairs={{0,32},{8,40},{16,48},{24,56},{32,0},{40,8},{48,16},{56,24},{64,96... | collective-permute-start | bytes 98312 | tf_op jit(solution)/shard_map/ppermute | solution.py:13
  64.3 10.5 %collective-permute-start.2 = (bf16[1,4,2,2048]{3,2,1,0:T(2,128)(2,1)S(1)}, bf16[1,4,2,2048]{3,2,1,0:T(2,128)(2,1)S(1)}, u32[]{:S(2)}, u32[]{:S(2)}) collective-permute-start(bf16[1,4,2,2048]{3,2,1,0:T(2,128)(2,1)S(1)} %bitcast.183), channel_id=1, source_target_pairs={{0,32},{8,40},{16,48},{24,56},{32,0},{40,8},{48,16},{56,24},{64,96... | collective-permute-start | bytes 98312 | tf_op jit(solution)/shard_map/ppermute | solution.py:13
  66.3 10.7 %collective-permute-start.18 = (bf16[1,4,2,2048]{3,2,1,0:T(2,128)(2,1)S(1)}, bf16[1,4,2,2048]{3,2,1,0:T(2,128)(2,1)S(1)}, u32[]{:S(2)}, u32[]{:S(2)}) collective-permute-start(bf16[1,4,2,2048]{3,2,1,0:T(2,128)(2,1)S(1)} %bitcast.184), channel_id=1, source_target_pairs={{0,64},{8,72},{16,80},{24,88},{32,96},{40,104},{48,112},{56,120},{... | collective-permute-start | bytes 98312 | tf_op jit(solution)/shard_map/ppermute | solution.py:13
  69.5 11.7 %collective-permute-start.13 = (bf16[1,4,2,2048]{3,2,1,0:T(2,128)(2,1)S(1)}, bf16[1,4,2,2048]{3,2,1,0:T(2,128)(2,1)S(1)}, u32[]{:S(2)}, u32[]{:S(2)}) collective-permute-start(bf16[1,4,2,2048]{3,2,1,0:T(2,128)(2,1)S(1)} %bitcast.185), channel_id=1, source_target_pairs={{0,64},{8,72},{16,80},{24,88},{32,96},{40,104},{48,112},{56,120},{... | collective-permute-start | bytes 98312 | tf_op jit(solution)/shard_map/ppermute | solution.py:13
  71.6 11.6 %collective-permute-start.8 = (bf16[1,4,2,2048]{3,2,1,0:T(2,128)(2,1)S(1)}, bf16[1,4,2,2048]{3,2,1,0:T(2,128)(2,1)S(1)}, u32[]{:S(2)}, u32[]{:S(2)}) collective-permute-start(bf16[1,4,2,2048]{3,2,1,0:T(2,128)(2,1)S(1)} %bitcast.186), channel_id=1, source_target_pairs={{0,64},{8,72},{16,80},{24,88},{32,96},{40,104},{48,112},{56,120},{... | collective-permute-start | bytes 98312 | tf_op jit(solution)/shard_map/ppermute | solution.py:13
  74.9 12.6 %collective-permute-start.3 = (bf16[1,4,2,2048]{3,2,1,0:T(2,128)(2,1)S(1)}, bf16[1,4,2,2048]{3,2,1,0:T(2,128)(2,1)S(1)}, u32[]{:S(2)}, u32[]{:S(2)}) collective-permute-start(bf16[1,4,2,2048]{3,2,1,0:T(2,128)(2,1)S(1)} %bitcast.187), channel_id=1, source_target_pairs={{0,64},{8,72},{16,80},{24,88},{32,96},{40,104},{48,112},{56,120},{... | collective-permute-start | bytes 98312 | tf_op jit(solution)/shard_map/ppermute | solution.py:13
  77.0 12.5 %collective-permute-start.19 = (bf16[1,4,2,2048]{3,2,1,0:T(2,128)(2,1)S(1)}, bf16[1,4,2,2048]{3,2,1,0:T(2,128)(2,1)S(1)}, u32[]{:S(2)}, u32[]{:S(2)}) collective-permute-start(bf16[1,4,2,2048]{3,2,1,0:T(2,128)(2,1)S(1)} %bitcast.188), channel_id=1, source_target_pairs={{0,128},{8,136},{16,144},{24,152},{32,160},{40,168},{48,176},{56,1... | collective-permute-start | bytes 98312 | tf_op jit(solution)/shard_map/ppermute | solution.py:13
  81.2 15.7 %collective-permute-start.14 = (bf16[1,4,2,2048]{3,2,1,0:T(2,128)(2,1)S(1)}, bf16[1,4,2,2048]{3,2,1,0:T(2,128)(2,1)S(1)}, u32[]{:S(2)}, u32[]{:S(2)}) collective-permute-start(bf16[1,4,2,2048]{3,2,1,0:T(2,128)(2,1)S(1)} %bitcast.189), channel_id=1, source_target_pairs={{0,128},{8,136},{16,144},{24,152},{32,160},{40,168},{48,176},{56,1... | collective-permute-start | bytes 98312 | tf_op jit(solution)/shard_map/ppermute | solution.py:13
  83.2 15.7 %collective-permute-start.9 = (bf16[1,4,2,2048]{3,2,1,0:T(2,128)(2,1)S(1)}, bf16[1,4,2,2048]{3,2,1,0:T(2,128)(2,1)S(1)}, u32[]{:S(2)}, u32[]{:S(2)}) collective-permute-start(bf16[1,4,2,2048]{3,2,1,0:T(2,128)(2,1)S(1)} %bitcast.190), channel_id=1, source_target_pairs={{0,128},{8,136},{16,144},{24,152},{32,160},{40,168},{48,176},{56,1... | collective-permute-start | bytes 98312 | tf_op jit(solution)/shard_map/ppermute | solution.py:13
  87.5 18.7 %collective-permute-start.4 = (bf16[1,4,2,2048]{3,2,1,0:T(2,128)(2,1)S(1)}, bf16[1,4,2,2048]{3,2,1,0:T(2,128)(2,1)S(1)}, u32[]{:S(2)}, u32[]{:S(2)}) collective-permute-start(bf16[1,4,2,2048]{3,2,1,0:T(2,128)(2,1)S(1)} %bitcast.191), channel_id=1, source_target_pairs={{0,128},{8,136},{16,144},{24,152},{32,160},{40,168},{48,176},{56,1... | collective-permute-start | bytes 98312 | tf_op jit(solution)/shard_map/ppermute | solution.py:13
  89.5 18.9 %collective-permute-start.20 = (bf16[1,4,2,2048]{3,2,1,0:T(2,128)(2,1)S(1)}, bf16[1,4,2,2048]{3,2,1,0:T(2,128)(2,1)S(1)}, u32[]{:S(2)}, u32[]{:S(2)}) collective-permute-start(bf16[1,4,2,2048]{3,2,1,0:T(2,128)(2,1)S(1)} %bitcast.192), channel_id=1, source_target_pairs={{0,256},{8,264},{16,272},{24,280},{32,288},{40,296},{48,304},{56,3... | collective-permute-start | bytes 98312 | tf_op jit(solution)/shard_map/ppermute | solution.py:13
  97.0 11.5 %collective-permute-start.15 = (bf16[1,4,2,2048]{3,2,1,0:T(2,128)(2,1)S(1)}, bf16[1,4,2,2048]{3,2,1,0:T(2,128)(2,1)S(1)}, u32[]{:S(2)}, u32[]{:S(2)}) collective-permute-start(bf16[1,4,2,2048]{3,2,1,0:T(2,128)(2,1)S(1)} %bitcast.193), channel_id=1, source_target_pairs={{0,256},{8,264},{16,272},{24,280},{32,288},{40,296},{48,304},{56,3... | collective-permute-start | bytes 98312 | tf_op jit(solution)/shard_map/ppermute | solution.py:13
  98.9 9.6 %collective-permute-start.10 = (bf16[1,4,2,2048]{3,2,1,0:T(2,128)(2,1)S(1)}, bf16[1,4,2,2048]{3,2,1,0:T(2,128)(2,1)S(1)}, u32[]{:S(2)}, u32[]{:S(2)}) collective-permute-start(bf16[1,4,2,2048]{3,2,1,0:T(2,128)(2,1)S(1)} %bitcast.194), channel_id=1, source_target_pairs={{0,256},{8,264},{16,272},{24,280},{32,288},{40,296},{48,304},{56,3... | collective-permute-start | bytes 98312 | tf_op jit(solution)/shard_map/ppermute | solution.py:13
  106.2 8.9 %collective-permute-start.5 = (bf16[1,4,2,2048]{3,2,1,0:T(2,128)(2,1)S(1)}, bf16[1,4,2,2048]{3,2,1,0:T(2,128)(2,1)S(1)}, u32[]{:S(2)}, u32[]{:S(2)}) collective-permute-start(bf16[1,4,2,2048]{3,2,1,0:T(2,128)(2,1)S(1)} %bitcast.195), channel_id=1, source_target_pairs={{0,256},{8,264},{16,272},{24,280},{32,288},{40,296},{48,304},{56,3... | collective-permute-start | bytes 98312 | tf_op jit(solution)/shard_map/ppermute | solution.py:13
Sparse Core Ops, SparseCore 0:
  137.6 78.7 all-reduce.2
where the time goes:
time: 228 us; the launch traced here: 225 us
  waiting for transfers between devices  83.6 us (37%)
  starting transfers between devices  80.9 us (35%)
  between operations  30.1 us (13%)
  matrix products  16.9 us (7%)
  local copies, waits for them, and re-layouts  6.7 us (3%)
  other arithmetic  6.52 us (3%)
    ppermute x21, starting transfers between devices, from_partner(): lax.ppermute(array, axis, [(i, i ^ 1 << bit) for i in range(lax.axis_size...  80.9 us
    unnamed x2, waiting for transfers between devices  77.1 us
    ppermute x21, waiting for transfers between devices, from_partner(): lax.ppermute(array, axis, [(i, i ^ 1 << bit) for i in range(lax.axis_size...  6.58 us
  transfers between devices with their start and end apart: 22, of which 2 were waited for; matrix products, arithmetic and copies ran while one was open for 1% of the time, Pallas kernels for 0%

commit v1 on v0

v1 whole, which is shorter than its diff:
```python
import functools
import math

import jax
import jax.numpy as jnp
import numpy as np
from jax import lax
from jax.experimental import pallas as pl
from jax.experimental.pallas import tpu as pltpu
from jax.sharding import Mesh, PartitionSpec as P

NFFT = 8192
MAXLAG = 1200
LANES = 128
STATIONS_HERE = 4
ROUNDS = 4
WINDOWS = 8
COARSE = 16
SHARES = 64
PAIR_LANES = 64
GROUPS = 19
GROUP_ROWS = 80
INTERPRET = False

VMEM = pltpu.MemorySpace.VMEM
SMEM = pltpu.MemorySpace.SMEM


def split_bf16(table):
    high = table.astype(jnp.bfloat16)
    low = (table - high.astype(np.float64)).astype(jnp.bfloat16)
    return high, low


@functools.lru_cache(None)
def selection_tables():
    lane = np.arange(LANES)
    coarse, station, part = lane // 8, lane // 2 % 4, lane % 2
    half, out_coarse, low, out_part = lane // 64, lane // 4 % 16, lane // 2 % 2, lane % 2
    same_bin = coarse[:, None] == out_coarse[None, :]
    own = [
        same_bin & (station == i)[:, None] & (part == c)[:, None]
        for c in range(2)
        for i in range(STATIONS_HERE)
    ]
    far_station = same_bin & (station[:, None] == (2 * half + low)[None, :])
    match = (part[:, None] == out_part[None, :]) & far_station
    cross = (part[:, None] != out_part[None, :]) & far_station
    sign = np.where(out_part == 1, -1.0, 1.0)
    return (
        np.concatenate(own, axis=1).astype(jnp.bfloat16),
        np.concatenate([match * sign, cross * 1.0], axis=1).astype(jnp.bfloat16),
    )


@functools.lru_cache(None)
def transform_tables():
    f = np.arange(LANES)
    shift = -MAXLAG % LANES
    base = (MAXLAG + shift) // LANES
    lane = np.arange(PAIR_LANES)
    coarse, pair, part = lane // 4, lane // 2 % 2, lane % 2
    angle = 2 * np.pi * (coarse[:, None] * (f + shift)[None, :] % 64) / 64
    cos, sin = np.cos(angle), np.sin(angle)
    real = np.where(part[:, None] == 0, cos, -sin)
    imag = np.where(part[:, None] == 0, sin, cos)
    first = np.concatenate(
        [
            np.where((pair == p)[:, None], value, 0.0)
            for p in range(2)
            for value in (real, imag)
        ],
        axis=1,
    )
    first = np.concatenate(split_bf16(first), axis=0)
    row = np.arange(SHARES * 8)
    fine = 2 * (row // 8) + row % 2
    twist = 2 * np.pi * (fine[:, None] * (f + shift)[None, :] % NFFT) / NFFT
    out_row = np.arange(GROUP_ROWS)
    group, out_round = out_row // ROUNDS, out_row % ROUNDS
    in_row = np.arange(SHARES // 2 * 8)
    in_fine, in_round = 2 * (in_row // 8) + in_row % 2, in_row // 2 % ROUNDS
    last = 2 * np.pi * (in_fine[None, :] * (group - base)[:, None] % 64) / 64
    keep = (out_round[:, None] == in_round[None, :]) & (group < GROUPS)[:, None]
    scale = 2.0 / math.sqrt(WINDOWS * COARSE * LANES)
    cos_hi, cos_lo = split_bf16(np.where(keep, np.cos(last) * scale, 0.0))
    sin_hi, sin_lo = split_bf16(np.where(keep, -np.sin(last) * scale, 0.0))
    return (
        first,
        np.cos(twist).astype(np.float32),
        np.sin(twist).astype(np.float32),
        np.stack([cos_hi, cos_lo, sin_hi, sin_lo]),
    )


def whiten_kernel(spectra_ref, out_ref, rows_ref):
    for station in range(STATIONS_HERE):
        value = spectra_ref[0, station]
        power = jnp.sum(value * value, axis=0, keepdims=True)
        level = jnp.mean(power, axis=1, keepdims=True)
        denom = jnp.sqrt(power + 0.05 * (level + 1e-06))
        white = value / denom
        for coarse in range(COARSE):
            rows_ref[pl.ds(coarse * 8 + station * 2, 2), :] = white[
                :, coarse * LANES : (coarse + 1) * LANES
            ]
    turned = rows_ref[...].T.astype(jnp.bfloat16)
    for copy in range(out_ref.shape[0]):
        out_ref[copy] = turned


def cross_kernel(mask_ref, home_ref, all_ref, own_table, far_table, out_ref, far_ref, left, right):
    home = home_ref[0]
    own = all_ref[pl.ds(pl.multiple_of(home * 128, 128), 128), :]
    left[...] = jnp.dot(own, own_table[...], preferred_element_type=jnp.float32)
    for r in range(ROUNDS):
        mask = mask_ref[r]
        high = (home ^ (mask >> 3)) & 7
        for block in range(8):
            other = (block ^ mask) & 7
            start = pl.multiple_of(high * 128 + other * 16, 16)
            far_ref[pl.ds(r * 128 + block * 16, 16), :] = all_ref[pl.ds(start, 16), :]
    right[...] = jnp.dot(far_ref[...], far_table[...], preferred_element_type=jnp.float32)
    sublane = lax.broadcasted_iota(jnp.int32, (8, LANES), 0)
    lower = lax.broadcasted_iota(jnp.int32, (8, LANES), 1) < PAIR_LANES

    for block in range(8):
        tiles = []
        for i in range(STATIONS_HERE):
            tile = None
            for r in range(ROUNDS):
                total = None
                for step in range(2):
                    rows = pl.ds(block * 16 + step * 8, 8)
                    far_rows = pl.ds(r * 128 + block * 16 + step * 8, 8)
                    for part in range(2):
                        term = (
                            left[rows, pl.ds((part * 4 + i) * LANES, LANES)]
                            * right[far_rows, pl.ds(part * LANES, LANES)]
                        )
                        total = term if total is None else total + term
                total = total + pltpu.roll(total, 4, 0)
                total = total + pltpu.roll(total, 2, 0)
                tile = total if tile is None else jnp.where(sublane >= 2 * r, total, tile)
            turned = pltpu.roll(tile, PAIR_LANES, 1)
            first = jnp.where(lower, tile, turned)
            second = jnp.where(lower, turned, tile)
            tiles += [first, second]
        for index, tile in enumerate(tiles):
            out_ref[block * 8 + index] = tile.astype(jnp.bfloat16)


def transform_kernel(spec_ref, first_ref, cos_ref, sin_ref, last_ref, out_ref, mid_ref):
    row = lax.broadcasted_iota(jnp.int32, (8, LANES), 0)
    lane = lax.broadcasted_iota(jnp.int32, (8, LANES), 1) % PAIR_LANES
    zero_bin = (row % 2 == 0) & (lane < 4)
    head = spec_ref[pl.ds(0, 8), :].astype(jnp.float32)
    head = jnp.where(zero_bin, 0.5 * head, head).astype(jnp.bfloat16)
    spec = jnp.concatenate([head, spec_ref[pl.ds(8, SHARES * 8 - 8), :]], axis=0)
    mid_ref[...] = jnp.dot(spec, first_ref[...], preferred_element_type=jnp.float32)
    half = SHARES * 4
    real, imag = [], []
    for pair in range(2):
        parts_re, parts_im = [], []
        for side in range(2):
            rows = pl.ds(side * half, half)
            y_re = mid_ref[rows, pl.ds(pair * 256, LANES)]
            y_im = mid_ref[rows, pl.ds(pair * 256 + LANES, LANES)]
            c, s = cos_ref[rows, :], sin_ref[rows, :]
            parts_re.append(y_re * c - y_im * s)
            parts_im.append(y_re * s + y_im * c)
        real.append(parts_re[0] + parts_re[1])
        imag.append(parts_im[0] + parts_im[1])
    total = None
    for index, value in ((0, jnp.concatenate(real, axis=1)), (2, jnp.concatenate(imag, axis=1))):
        high = value.astype(jnp.bfloat16)
        low = (value - high.astype(jnp.float32)).astype(jnp.bfloat16)
        for table, operand in ((index, high), (index + 1, high), (index, low)):
            term = jnp.dot(last_ref[table], operand, preferred_element_type=jnp.float32)
            total = term if total is None else total + term
    lags = out_ref.shape[2]
    for pair in range(2):
        for group in range(GROUPS):
            width = min(LANES, lags - group * LANES)
            out_ref[pair, :, pl.ds(group * LANES, width)] = total[
                group * ROUNDS : (group + 1) * ROUNDS, pair * LANES : pair * LANES + width
            ]


def spec_of(space):
    return pl.BlockSpec(memory_space=space)


def whiten(spectra, copies):
    return pl.pallas_call(
        whiten_kernel,
        out_shape=jax.ShapeDtypeStruct((copies, LANES, LANES), jnp.bfloat16),
        in_specs=[spec_of(VMEM)],
        out_specs=spec_of(VMEM),
        scratch_shapes=[pltpu.VMEM((LANES, LANES), jnp.float32)],
        name="whiten",
        interpret=INTERPRET,
    )(spectra)


def cross(partner_masks, home, gathered):
    own_table, far_table = selection_tables()
    return pl.pallas_call(
        cross_kernel,
        out_shape=jax.ShapeDtypeStruct((SHARES, 8, LANES), jnp.bfloat16),
        in_specs=[spec_of(SMEM)] * 2 + [spec_of(VMEM)] * 3,
        out_specs=spec_of(VMEM),
        scratch_shapes=[
            pltpu.VMEM((512, LANES), jnp.bfloat16),
            pltpu.VMEM((LANES, 1024), jnp.float32),
            pltpu.VMEM((512, 256), jnp.float32),
        ],
        name="cross",
        interpret=INTERPRET,
    )(partner_masks, home, gathered, jnp.asarray(own_table), jnp.asarray(far_table))


def transform(spec_rows):
    tables = [jnp.asarray(table) for table in transform_tables()]
    return pl.pallas_call(
        transform_kernel,
        out_shape=jax.ShapeDtypeStruct((2, ROUNDS, 2 * MAXLAG), jnp.float32),
        in_specs=[spec_of(VMEM)] * 5,
        out_specs=spec_of(VMEM),
        scratch_shapes=[pltpu.VMEM((SHARES * 8, 512), jnp.float32)],
        name="transform",
        interpret=INTERPRET,
    )(spec_rows, *tables)


def body(spectra, partner_masks):
    rows = whiten(spectra, lax.axis_size("high"))
    slots = rows.reshape(512, 2, LANES)
    gathered = lax.all_to_all(slots, ("high", "low", "stk"), 0, 0, tiled=True)
    home = lax.axis_index("high").astype(jnp.int32).reshape(1)
    spec = cross(partner_masks, home, gathered.reshape(1024, LANES))
    owned = lax.all_to_all(spec, ("low", "stk"), 0, 0, tiled=True)
    return transform(owned.reshape(SHARES * 8, LANES))


def solution(mesh):
    devices = mesh.devices
    fine = Mesh(devices.reshape(8, devices.shape[0] // 8, devices.shape[1]), ("high", "low", "stk"))
    return jax.shard_map(
        body,
        mesh=fine,
        in_specs=(P("stk", ("high", "low"), None, None), P()),
        out_specs=P(("high", "low", "stk"), None, None),
        check_vma=False,
    )
```

time: 228 us -> 64.4 us (0.28); the launches traced: 225 us -> 64.1 us
  waiting for transfers between devices: 83.6 us -> 17.4 us
  starting transfers between devices: 80.9 us -> 22.1 us
  between operations: 30.1 us -> 0.02 us
  blocking collectives: 0 us -> 17.3 us
  matrix products: 16.9 us -> 0 us
  Pallas kernels: 0 us -> 6.58 us
  other arithmetic: 6.52 us -> 0 us
  local copies, waits for them, and re-layouts: 6.7 us -> 0.69 us
    ppermute x21 -> x0, starting transfers between devices: 80.9 us -> none  [from_partner(): lax.ppermute(array, axis, [(i, i ^ 1 << bit) for i in range(lax.axis_size...]
    unnamed x2 -> x0, waiting for transfers between devices: 77.1 us -> none
    all_to_all x0 -> x1, starting transfers between devices: none -> 22.1 us  [body(): gathered = lax.all_to_all(slots, ('high', 'low', 'stk'), 0, 0, tiled=True)]
    all_to_all x0 -> x1, waiting for transfers between devices: none -> 17.4 us  [body(): gathered = lax.all_to_all(slots, ('high', 'low', 'stk'), 0, 0, tiled=True)]
    all_to_all x0 -> x1, blocking collectives: none -> 17.3 us  [body(): owned = lax.all_to_all(spec, ('low', 'stk'), 0, 0, tiled=True)]
    dot_general x6 -> x0, matrix products: 16.9 us -> none  [the longest x1 3.71 us: transform(): jnp.einsum('rac,af->rcf', rotated_im, first_sin, precision=highest)]
    ppermute x21 -> x0, waiting for transfers between devices: 6.58 us -> none  [from_partner(): lax.ppermute(array, axis, [(i, i ^ 1 << bit) for i in range(lax.axis_size...]
    pallas_call x0 -> x3, Pallas kernels: none -> 6.58 us  [the longest x1 2.53 us: transform(): pl.pallas_call(transform_kernel, out_shape=jax.ShapeDtypeStruct((2, ROUND...]
  transfers between devices with their start and end apart: 22 -> 1, of which waited for: 2 -> 1; matrix products, arithmetic and copies ran while one was open for 1% -> 0% of each run, Pallas kernels for 0% -> 0%
where the time goes in v1:
time: 64.4 us; the launch traced here: 64.1 us
  starting transfers between devices  22.1 us (34%)
  waiting for transfers between devices  17.4 us (27%)
  blocking collectives  17.3 us (27%)
  Pallas kernels  6.58 us (10%)
  local copies, waits for them, and re-layouts  0.69 us (1%)
    all_to_all x1, starting transfers between devices, body(): gathered = lax.all_to_all(slots, ('high', 'low', 'stk'), 0, 0, tiled=True)  22.1 us
    all_to_all x1, waiting for transfers between devices, body(): gathered = lax.all_to_all(slots, ('high', 'low', 'stk'), 0, 0, tiled=True)  17.4 us
    all_to_all x1, blocking collectives, body(): owned = lax.all_to_all(spec, ('low', 'stk'), 0, 0, tiled=True)  17.3 us
    pallas_call x1, Pallas kernels, transform(): pl.pallas_call(transform_kernel, out_shape=jax.ShapeDtypeStruct((2, ROUND...  2.53 us
    pallas_call x1, Pallas kernels, cross(): pl.pallas_call(cross_kernel, out_shape=jax.ShapeDtypeStruct((SHARES, 8, L...  2.22 us
    pallas_call x1, Pallas kernels, whiten(): pl.pallas_call(whiten_kernel, out_shape=jax.ShapeDtypeStruct((copies, LAN...  1.83 us
  transfers between devices with their start and end apart: 1, of which 1 were waited for; matrix products, arithmetic and copies ran while one was open for 0% of the time, Pallas kernels for 0%

profile of v1, /device:TPU:1, one launch (start us, length us, event | category | flops | bytes accessed | tf_op | source)
XLA Modules:
  0.0 64.1 jit_solution(8520516638023503772)
XLA Ops:
  0.0 1.8 %whiten.1 = bf16[8,128,128]{2,1,0:T(8,128)(2,1)} custom-call(f32[1,4,2,2048]{3,2,1,0:T(2,128)} %spectra_ref.1), custom_call_target="tpu_custom_call" | custom-call | tf_op jit(solution)/shard_map/whiten/pallas_call | solution.py:195
  1.8 22.1 %all-to-all-start = ((bf16[512,2,128]{2,1,0:T(2,128)(2,1)}), bf16[512,2,128]{2,1,0:T(2,128)(2,1)S(1)}, u32[]{:S(2)}, u32[]{:S(2)}) async-start(bf16[512,2,128]{2,1,0:T(2,128)(2,1)} %bitcast.4), calls=%async_computation | async-start | bytes 524288 | tf_op jit(solution)/shard_map/all_to_all | solution.py:239
  24.0 17.4 %all-to-all-done = bf16[512,2,128]{2,1,0:T(2,128)(2,1)S(1)} async-done(((bf16[512,2,128]{2,1,0:T(2,128)(2,1)}), bf16[512,2,128]{2,1,0:T(2,128)(2,1)S(1)}, u32[]{:S(2)}, u32[]{:S(2)}) %all-to-all-start) | async-done | bytes 262176 | tf_op jit(solution)/shard_map/all_to_all | solution.py:239
  41.3 0.0 copy-start
  41.3 0.7 %copy-done = bf16[512,2,128]{2,1,0:T(2,128)(2,1)} copy-done((bf16[512,2,128]{2,1,0:T(2,128)(2,1)}, bf16[512,2,128]{2,1,0:T(2,128)(2,1)S(1)}, u32[]{:S(2)}) %copy-start) | copy-done | bytes 262168
  42.0 2.2 %cross.1 = bf16[64,8,128]{2,1,0:T(8,128)(2,1)} custom-call(s32[4]{0:T(128)} %mask_ref.1, s32[1]{0:T(128)} %bitcast.home_ref, bf16[1024,128]{1,0:T(8,128)(2,1)} %bitcast.5, bf16[128,1024]{1,0:T(8,128)(2,1)} %constant.18.clone.own_table, bf16[128,256]{1,0:T(8,128)(2,1)} %constant.19.clone.far_table), custom_call_target="tpu_custom_call" | custom-call | tf_op jit(solution)/shard_map/cross/pallas_call | solution.py:208
  44.3 17.3 %all_to_all.10 = bf16[64,8,128]{2,1,0:T(8,128)(2,1)} all-to-all(bf16[64,8,128]{2,1,0:T(8,128)(2,1)} %cross.1), channel_id=1, replica_groups=mesh['high'=8,'low'=8,'stk'=8] {'low','stk'}, dimensions={0} | all-to-all | bytes 262144 | tf_op jit(solution)/shard_map/all_to_all | solution.py:242
  61.5 2.5 %transform.1 = f32[2,4,2400]{2,1,0:T(4,128)} custom-call(bf16[512,128]{1,0:T(8,128)(2,1)} %bitcast.6, bf16[128,512]{1,0:T(8,128)(2,1)} %constant.20.clone.first_ref, f32[512,128]{1,0:T(8,128)} %constant.21.clone.cos_ref, f32[512,128]{1,0:T(8,128)} %constant.22.clone.sin_ref, bf16[4,80,256]{2,1,0:T(8,128)(2,1)} %constant.23.clone.last_ref), custom_call_target="tpu_custom_call" | custom-call | tf_op jit(solution)/shard_map/transform/pallas_call | solution.py:225
Async XLA Ops:
  1.8 39.5 %all-to-all-start = ((bf16[512,2,128]{2,1,0:T(2,128)(2,1)}), bf16[512,2,128]{2,1,0:T(2,128)(2,1)S(1)}, u32[]{:S(2)}, u32[]{:S(2)}) async-start(bf16[512,2,128]{2,1,0:T(2,128)(2,1)} %bitcast.4), calls=%async_computation | async-start | bytes 524288 | tf_op jit(solution)/shard_map/all_to_all | solution.py:239
  41.3 0.7 %copy-start = (bf16[512,2,128]{2,1,0:T(2,128)(2,1)}, bf16[512,2,128]{2,1,0:T(2,128)(2,1)S(1)}, u32[]{:S(2)}) copy-start(bf16[512,2,128]{2,1,0:T(2,128)(2,1)S(1)} %all-to-all-done) | copy-start | bytes 786436

commit v2 on v1

--- a/solution.py
+++ b/solution.py
@@ -191,10 +191,14 @@
     return pl.BlockSpec(memory_space=space)
 
 
+def in_vmem(array):
+    return pltpu.with_memory_space_constraint(jnp.asarray(array), VMEM)
+
+
 def whiten(spectra, copies):
     return pl.pallas_call(
         whiten_kernel,
-        out_shape=jax.ShapeDtypeStruct((copies, LANES, LANES), jnp.bfloat16),
+        out_shape=pltpu.VMEM((copies, LANES, LANES), jnp.bfloat16),
         in_specs=[spec_of(VMEM)],
         out_specs=spec_of(VMEM),
         scratch_shapes=[pltpu.VMEM((LANES, LANES), jnp.float32)],
@@ -207,7 +211,7 @@
     own_table, far_table = selection_tables()
     return pl.pallas_call(
         cross_kernel,
-        out_shape=jax.ShapeDtypeStruct((SHARES, 8, LANES), jnp.bfloat16),
+        out_shape=pltpu.VMEM((SHARES, 8, LANES), jnp.bfloat16),
         in_specs=[spec_of(SMEM)] * 2 + [spec_of(VMEM)] * 3,
         out_specs=spec_of(VMEM),
         scratch_shapes=[
@@ -217,11 +221,10 @@
         ],
         name="cross",
         interpret=INTERPRET,
-    )(partner_masks, home, gathered, jnp.asarray(own_table), jnp.asarray(far_table))
+    )(partner_masks, home, *map(in_vmem, (gathered, own_table, far_table)))
 
 
 def transform(spec_rows):
-    tables = [jnp.asarray(table) for table in transform_tables()]
     return pl.pallas_call(
         transform_kernel,
         out_shape=jax.ShapeDtypeStruct((2, ROUNDS, 2 * MAXLAG), jnp.float32),
@@ -230,7 +233,7 @@
         scratch_shapes=[pltpu.VMEM((SHARES * 8, 512), jnp.float32)],
         name="transform",
         interpret=INTERPRET,
-    )(spec_rows, *tables)
+    )(*map(in_vmem, (spec_rows, *transform_tables())))
 
 
 def body(spectra, partner_masks):

time: 64.4 us -> 61.2 us (0.950)
  Pallas kernels: 6.58 us -> 4.47 us
  local copies, waits for them, and re-layouts: 0.69 us -> 0.03 us
    pallas_call x1, Pallas kernels: 2.53 us -> 1.32 us  [transform(): pl.pallas_call(transform_kernel, out_shape=jax.ShapeDtypeStruct((2, ROUND...]
    pallas_call x2, Pallas kernels: 4.05 us -> 3.14 us  [the longest x1 1.84 us: whiten(): pl.pallas_call(whiten_kernel, out_shape=pltpu.VMEM((copies, LANES, LANES)...]
    unnamed x2 -> x12, local copies, waits for them, and re-layouts: 0.69 us -> 0.03 us
where the time goes in v2:
time: 61.2 us; the launch traced here: 61 us
  starting transfers between devices  22.1 us (36%)
  waiting for transfers between devices  17.3 us (28%)
  blocking collectives  17 us (28%)
  Pallas kernels  4.47 us (7%)
    all_to_all x1, starting transfers between devices, body(): gathered = lax.all_to_all(slots, ('high', 'low', 'stk'), 0, 0, tiled=True)  22.1 us
    all_to_all x1, waiting for transfers between devices, body(): gathered = lax.all_to_all(slots, ('high', 'low', 'stk'), 0, 0, tiled=True)  17.3 us
    all_to_all x1, blocking collectives, body(): owned = lax.all_to_all(spec, ('low', 'stk'), 0, 0, tiled=True)  17 us
    pallas_call x1, Pallas kernels, whiten(): pl.pallas_call(whiten_kernel, out_shape=pltpu.VMEM((copies, LANES, LANES)...  1.84 us
    pallas_call x1, Pallas kernels, transform(): pl.pallas_call(transform_kernel, out_shape=jax.ShapeDtypeStruct((2, ROUND...  1.32 us
    pallas_call x1, Pallas kernels, cross(): pl.pallas_call(cross_kernel, out_shape=pltpu.VMEM((SHARES, 8, LANES), jnp...  1.3 us
  transfers between devices with their start and end apart: 1, of which 1 were waited for; matrix products, arithmetic and copies ran while one was open for 0% of the time, Pallas kernels for 0%

profile of v2, /device:TPU:1, one launch (start us, length us, event | category | flops | bytes accessed | tf_op | source)
XLA Modules:
  0.0 61.0 jit_solution(14151836242025327066)
XLA Ops:
  0.0 1.8 %whiten.1 = bf16[8,128,128]{2,1,0:T(8,128)(2,1)} custom-call(f32[1,4,2,2048]{3,2,1,0:T(2,128)} %spectra_ref.1), custom_call_target="tpu_custom_call" | custom-call | tf_op jit(solution)/shard_map/whiten/pallas_call | solution.py:199
  1.8 0.0 copy-start
  1.8 0.0 copy-start.5
  1.8 22.1 %all-to-all-start = ((bf16[512,2,128]{2,1,0:T(2,128)(2,1)}), bf16[512,2,128]{2,1,0:T(2,128)(2,1)S(1)}, u32[]{:S(2)}, u32[]{:S(2)}) async-start(bf16[512,2,128]{2,1,0:T(2,128)(2,1)} %bitcast.1), calls=%async_computation | async-start | bytes 524288 | tf_op jit(solution)/shard_map/all_to_all | solution.py:242
  24.0 17.3 %all-to-all-done = bf16[512,2,128]{2,1,0:T(2,128)(2,1)S(1)} async-done(((bf16[512,2,128]{2,1,0:T(2,128)(2,1)}), bf16[512,2,128]{2,1,0:T(2,128)(2,1)S(1)}, u32[]{:S(2)}, u32[]{:S(2)}) %all-to-all-start) | async-done | bytes 262176 | tf_op jit(solution)/shard_map/all_to_all | solution.py:242
  41.3 0.0 copy-done
  41.3 0.0 copy-done.5
  41.4 0.0 copy-start.2
  41.4 0.0 copy-start.3
  41.4 0.0 copy-start.4
  41.4 1.3 %cross.1 = bf16[64,8,128]{2,1,0:T(8,128)(2,1)S(1)} custom-call(s32[4]{0:T(128)} %mask_ref.1, s32[1]{0:T(128)} %bitcast.home_ref, bf16[1024,128]{1,0:T(8,128)(2,1)S(1)} %bitcast.4, bf16[128,1024]{1,0:T(8,128)(2,1)S(1)} %copy-done, bf16[128,256]{1,0:T(8,128)(2,1)S(1)} %copy-done.5), custom_call_target="tpu_custom_call" | custom-call | tf_op jit(solution)/shard_map/cross/pallas_call | solution.py:212
  42.7 0.0 copy-start.1
  42.7 17.0 %all_to_all.10 = bf16[64,8,128]{2,1,0:T(8,128)(2,1)S(1)} all-to-all(bf16[64,8,128]{2,1,0:T(8,128)(2,1)S(1)} %cross.1), channel_id=1, replica_groups=mesh['high'=8,'low'=8,'stk'=8] {'low','stk'}, dimensions={0} | all-to-all | bytes 262144 | tf_op jit(solution)/shard_map/all_to_all | solution.py:245
  59.7 0.0 copy-done.2
  59.7 0.0 copy-done.3
  59.7 0.0 copy-done.4
  59.7 0.0 copy-done.1
  59.7 1.3 %transform.1 = f32[2,4,2400]{2,1,0:T(4,128)} custom-call(bf16[512,128]{1,0:T(8,128)(2,1)S(1)} %bitcast.5, bf16[128,512]{1,0:T(8,128)(2,1)S(1)} %copy-done.4, f32[512,128]{1,0:T(8,128)S(1)} %copy-done.1, f32[512,128]{1,0:T(8,128)S(1)} %copy-done.2, bf16[4,80,256]{2,1,0:T(8,128)(2,1)S(1)} %copy-done.3), custom_call_target="tpu_custom_call" | custom-call | tf_op jit(solution)/shard_map/transform/pallas_call | solution.py:228
Async XLA Ops:
  1.8 39.5 %copy-start = (bf16[128,1024]{1,0:T(8,128)(2,1)S(1)}, bf16[128,1024]{1,0:T(8,128)(2,1)}, u32[]{:S(2)}) copy-start(bf16[128,1024]{1,0:T(8,128)(2,1)} %constant.18.clone.own_table) | copy-start | bytes 786436
  1.8 39.5 %copy-start.5 = (bf16[128,256]{1,0:T(8,128)(2,1)S(1)}, bf16[128,256]{1,0:T(8,128)(2,1)}, u32[]{:S(2)}) copy-start(bf16[128,256]{1,0:T(8,128)(2,1)} %constant.19.clone.far_table) | copy-start | bytes 196612
  1.8 39.5 %all-to-all-start = ((bf16[512,2,128]{2,1,0:T(2,128)(2,1)}), bf16[512,2,128]{2,1,0:T(2,128)(2,1)S(1)}, u32[]{:S(2)}, u32[]{:S(2)}) async-start(bf16[512,2,128]{2,1,0:T(2,128)(2,1)} %bitcast.1), calls=%async_computation | async-start | bytes 524288 | tf_op jit(solution)/shard_map/all_to_all | solution.py:242
  41.4 18.3 %copy-start.2 = (f32[512,128]{1,0:T(8,128)S(1)}, f32[512,128]{1,0:T(8,128)}, u32[]{:S(2)}) copy-start(f32[512,128]{1,0:T(8,128)} %constant.22.clone.sin_ref) | copy-start | bytes 786436
  41.4 18.3 %copy-start.3 = (bf16[4,80,256]{2,1,0:T(8,128)(2,1)S(1)}, bf16[4,80,256]{2,1,0:T(8,128)(2,1)}, u32[]{:S(2)}) copy-start(bf16[4,80,256]{2,1,0:T(8,128)(2,1)} %constant.23.clone.last_ref) | copy-start | bytes 491524
  41.4 18.3 %copy-start.4 = (bf16[128,512]{1,0:T(8,128)(2,1)S(1)}, bf16[128,512]{1,0:T(8,128)(2,1)}, u32[]{:S(2)}) copy-start(bf16[128,512]{1,0:T(8,128)(2,1)} %constant.20.clone.first_ref) | copy-start | bytes 393220
  42.7 17.0 %copy-start.1 = (f32[512,128]{1,0:T(8,128)S(1)}, f32[512,128]{1,0:T(8,128)}, u32[]{:S(2)}) copy-start(f32[512,128]{1,0:T(8,128)} %constant.21.clone.cos_ref) | copy-start | bytes 786436

commit v3 on v2

--- a/solution.py
+++ b/solution.py
@@ -16,7 +16,8 @@
 ROUNDS = 4
 WINDOWS = 8
 COARSE = 16
-SHARES = 64
+SHARES = 32
+SLOTS = 64
 PAIR_LANES = 64
 GROUPS = 19
 GROUP_ROWS = 80
@@ -58,28 +59,32 @@
     f = np.arange(LANES)
     shift = -MAXLAG % LANES
     base = (MAXLAG + shift) // LANES
-    lane = np.arange(PAIR_LANES)
-    coarse, pair, part = lane // 4, lane // 2 % 2, lane % 2
+    lane = np.arange(LANES)
+    in_bit, coarse, pair, part = lane // 64, lane // 4 % 16, lane // 2 % 2, lane % 2
     angle = 2 * np.pi * (coarse[:, None] * (f + shift)[None, :] % 64) / 64
     cos, sin = np.cos(angle), np.sin(angle)
     real = np.where(part[:, None] == 0, cos, -sin)
     imag = np.where(part[:, None] == 0, sin, cos)
     first = np.concatenate(
         [
-            np.where((pair == p)[:, None], value, 0.0)
+            np.where(((pair == p) & (in_bit == bit))[:, None], value, 0.0)
+            for bit in range(2)
             for p in range(2)
             for value in (real, imag)
         ],
         axis=1,
     )
-    first = np.concatenate(split_bf16(first), axis=0)
+    first_hi, first_lo = split_bf16(first)
+    first = np.concatenate([first_hi, first_hi, first_lo], axis=0)
     row = np.arange(SHARES * 8)
-    fine = 2 * (row // 8) + row % 2
-    twist = 2 * np.pi * (fine[:, None] * (f + shift)[None, :] % NFFT) / NFFT
+    fine = 4 * (row // 8) + row % 2
+    fine = np.repeat(np.stack([fine, fine + 2], axis=1), LANES, axis=1)
+    twist = 2 * np.pi * (fine * np.tile(f + shift, 2)[None, :] % NFFT) / NFFT
     out_row = np.arange(GROUP_ROWS)
     group, out_round = out_row // ROUNDS, out_row % ROUNDS
-    in_row = np.arange(SHARES // 2 * 8)
-    in_fine, in_round = 2 * (in_row // 8) + in_row % 2, in_row // 2 % ROUNDS
+    in_row = np.arange(SHARES * 8)
+    in_fine = 4 * (in_row // 8 % 16) + 2 * (in_row // 128) + in_row % 2
+    in_round = in_row // 2 % ROUNDS
     last = 2 * np.pi * (in_fine[None, :] * (group - base)[:, None] % 64) / 64
     keep = (out_round[:, None] == in_round[None, :]) & (group < GROUPS)[:, None]
     scale = 2.0 / math.sqrt(WINDOWS * COARSE * LANES)
@@ -95,16 +100,25 @@
 
 def whiten_kernel(spectra_ref, out_ref, rows_ref):
     for station in range(STATIONS_HERE):
-        value = spectra_ref[0, station]
-        power = jnp.sum(value * value, axis=0, keepdims=True)
-        level = jnp.mean(power, axis=1, keepdims=True)
-        denom = jnp.sqrt(power + 0.05 * (level + 1e-06))
-        white = value / denom
         for coarse in range(COARSE):
-            rows_ref[pl.ds(coarse * 8 + station * 2, 2), :] = white[
-                :, coarse * LANES : (coarse + 1) * LANES
+            rows_ref[pl.ds(coarse * 8 + station * 2, 2), :] = spectra_ref[
+                0, station, :, pl.ds(coarse * LANES, LANES)
             ]
-    turned = rows_ref[...].T.astype(jnp.bfloat16)
+    even = lax.broadcasted_iota(jnp.int32, (8, LANES), 0) % 2 == 0
+    power, total = [], None
+    for coarse in range(COARSE):
+        value = rows_ref[pl.ds(coarse * 8, 8), :]
+        square = value * value
+        other = jnp.where(even, pltpu.roll(square, 7, 0), pltpu.roll(square, 1, 0))
+        power.append(square + other)
+        total = power[-1] if total is None else total + power[-1]
+    level = jnp.sum(total, axis=1, keepdims=True) * (1.0 / (COARSE * LANES))
+    water = 0.05 * (level + 1e-06)
+    white = [
+        rows_ref[pl.ds(coarse * 8, 8), :] * lax.rsqrt(power[coarse] + water)
+        for coarse in range(COARSE)
+    ]
+    turned = jnp.concatenate(white, axis=0).T.astype(jnp.bfloat16)
     for copy in range(out_ref.shape[0]):
         out_ref[copy] = turned
 
@@ -122,12 +136,12 @@
             far_ref[pl.ds(r * 128 + block * 16, 16), :] = all_ref[pl.ds(start, 16), :]
     right[...] = jnp.dot(far_ref[...], far_table[...], preferred_element_type=jnp.float32)
     sublane = lax.broadcasted_iota(jnp.int32, (8, LANES), 0)
+    odd_round = sublane // 2 % 2 == 1
     lower = lax.broadcasted_iota(jnp.int32, (8, LANES), 1) < PAIR_LANES
 
     for block in range(8):
-        tiles = []
         for i in range(STATIONS_HERE):
-            tile = None
+            straight = crossed = None
             for r in range(ROUNDS):
                 total = None
                 for step in range(2):
@@ -140,41 +154,60 @@
                         )
                         total = term if total is None else total + term
                 total = total + pltpu.roll(total, 4, 0)
-                total = total + pltpu.roll(total, 2, 0)
-                tile = total if tile is None else jnp.where(sublane >= 2 * r, total, tile)
-            turned = pltpu.roll(tile, PAIR_LANES, 1)
-            first = jnp.where(lower, tile, turned)
-            second = jnp.where(lower, turned, tile)
-            tiles += [first, second]
-        for index, tile in enumerate(tiles):
-            out_ref[block * 8 + index] = tile.astype(jnp.bfloat16)
+                moved = pltpu.roll(total, 2, 0)
+                straight = total if r == 0 else jnp.where(sublane >= 2 * r, total, straight)
+                crossed = moved if r == 0 else jnp.where(sublane >= 2 * r, moved, crossed)
+            first = jnp.where(odd_round, crossed, straight)
+            second = jnp.where(odd_round, straight, crossed)
+            slot = block * 8 + i * 2
+            out_ref[slot] = jnp.where(
+                lower, first, pltpu.roll(second, PAIR_LANES, 1)
+            ).astype(jnp.bfloat16)
+            out_ref[slot + 1] = jnp.where(
+                lower, pltpu.roll(first, PAIR_LANES, 1), second
+            ).astype(jnp.bfloat16)
+
+
+def split_value(value):
+    high = value.astype(jnp.bfloat16)
+    return high, (value - high.astype(jnp.float32)).astype(jnp.bfloat16)
 
 
 def transform_kernel(spec_ref, first_ref, cos_ref, sin_ref, last_ref, out_ref, mid_ref):
-    row = lax.broadcasted_iota(jnp.int32, (8, LANES), 0)
-    lane = lax.broadcasted_iota(jnp.int32, (8, LANES), 1) % PAIR_LANES
-    zero_bin = (row % 2 == 0) & (lane < 4)
-    head = spec_ref[pl.ds(0, 8), :].astype(jnp.float32)
-    head = jnp.where(zero_bin, 0.5 * head, head).astype(jnp.bfloat16)
-    spec = jnp.concatenate([head, spec_ref[pl.ds(8, SHARES * 8 - 8), :]], axis=0)
-    mid_ref[...] = jnp.dot(spec, first_ref[...], preferred_element_type=jnp.float32)
+    both = spec_ref[...].astype(jnp.float32).reshape(SHARES, 2, 8, LANES)
+    spec = both[:, 0] + both[:, 1]
+    share = lax.broadcasted_iota(jnp.int32, spec.shape, 0)
+    row = lax.broadcasted_iota(jnp.int32, spec.shape, 1)
+    lane = lax.broadcasted_iota(jnp.int32, spec.shape, 2)
+    zero_bin = (share == 0) & (row % 2 == 0) & (lane < 4)
+    spec = jnp.where(zero_bin, 0.5 * spec, spec).reshape(SHARES * 8, LANES)
+    high, low = split_value(spec)
+    mid_ref[...] = jnp.dot(
+        jnp.concatenate([high, low, high], axis=1),
+        first_ref[...],
+        preferred_element_type=jnp.float32,
+    )
     half = SHARES * 4
     real, imag = [], []
     for pair in range(2):
-        parts_re, parts_im = [], []
-        for side in range(2):
-            rows = pl.ds(side * half, half)
-            y_re = mid_ref[rows, pl.ds(pair * 256, LANES)]
-            y_im = mid_ref[rows, pl.ds(pair * 256 + LANES, LANES)]
-            c, s = cos_ref[rows, :], sin_ref[rows, :]
-            parts_re.append(y_re * c - y_im * s)
-            parts_im.append(y_re * s + y_im * c)
-        real.append(parts_re[0] + parts_re[1])
-        imag.append(parts_im[0] + parts_im[1])
+        column_re, column_im = [], []
+        for bit in range(2):
+            parts_re, parts_im = [], []
+            for side in range(2):
+                rows = pl.ds(side * half, half)
+                y_re = mid_ref[rows, pl.ds((bit * 4 + pair * 2) * LANES, LANES)]
+                y_im = mid_ref[rows, pl.ds((bit * 4 + pair * 2 + 1) * LANES, LANES)]
+                c = cos_ref[rows, pl.ds(bit * LANES, LANES)]
+                s = sin_ref[rows, pl.ds(bit * LANES, LANES)]
+                parts_re.append(y_re * c - y_im * s)
+                parts_im.append(y_re * s + y_im * c)
+            column_re.append(parts_re[0] + parts_re[1])
+            column_im.append(parts_im[0] + parts_im[1])
+        real.append(jnp.concatenate(column_re, axis=0))
+        imag.append(jnp.concatenate(column_im, axis=0))
     total = None
     for index, value in ((0, jnp.concatenate(real, axis=1)), (2, jnp.concatenate(imag, axis=1))):
-        high = value.astype(jnp.bfloat16)
-        low = (value - high.astype(jnp.float32)).astype(jnp.bfloat16)
+        high, low = split_value(value)
         for table, operand in ((index, high), (index + 1, high), (index, low)):
             term = jnp.dot(last_ref[table], operand, preferred_element_type=jnp.float32)
             total = term if total is None else total + term
@@ -211,7 +244,7 @@
     own_table, far_table = selection_tables()
     return pl.pallas_call(
         cross_kernel,
-        out_shape=pltpu.VMEM((SHARES, 8, LANES), jnp.bfloat16),
+        out_shape=pltpu.VMEM((SLOTS, 8, LANES), jnp.bfloat16),
         in_specs=[spec_of(SMEM)] * 2 + [spec_of(VMEM)] * 3,
         out_specs=spec_of(VMEM),
         scratch_shapes=[
@@ -230,7 +263,7 @@
         out_shape=jax.ShapeDtypeStruct((2, ROUNDS, 2 * MAXLAG), jnp.float32),
         in_specs=[spec_of(VMEM)] * 5,
         out_specs=spec_of(VMEM),
-        scratch_shapes=[pltpu.VMEM((SHARES * 8, 512), jnp.float32)],
+        scratch_shapes=[pltpu.VMEM((SHARES * 8, 1024), jnp.float32)],
         name="transform",
         interpret=INTERPRET,
     )(*map(in_vmem, (spec_rows, *transform_tables())))
@@ -238,21 +271,25 @@
 
 def body(spectra, partner_masks):
     rows = whiten(spectra, lax.axis_size("high"))
-    slots = rows.reshape(512, 2, LANES)
-    gathered = lax.all_to_all(slots, ("high", "low", "stk"), 0, 0, tiled=True)
+    gathered = lax.all_to_all(
+        rows.reshape(256, 4, LANES), ("high", "low", "near"), 0, 0, tiled=True
+    )
     home = lax.axis_index("high").astype(jnp.int32).reshape(1)
     spec = cross(partner_masks, home, gathered.reshape(1024, LANES))
-    owned = lax.all_to_all(spec, ("low", "stk"), 0, 0, tiled=True)
-    return transform(owned.reshape(SHARES * 8, LANES))
+    owned = lax.all_to_all(spec, ("low", "near", "core"), 0, 0, tiled=True)
+    return transform(owned.reshape(SLOTS * 8, LANES))
 
 
 def solution(mesh):
     devices = mesh.devices
-    fine = Mesh(devices.reshape(8, devices.shape[0] // 8, devices.shape[1]), ("high", "low", "stk"))
+    fine = Mesh(
+        devices.reshape(8, devices.shape[0] // 8, devices.shape[1] // 2, 2),
+        ("high", "low", "near", "core"),
+    )
     return jax.shard_map(
         body,
         mesh=fine,
-        in_specs=(P("stk", ("high", "low"), None, None), P()),
-        out_specs=P(("high", "low", "stk"), None, None),
+        in_specs=(P(("near", "core"), ("high", "low"), None, None), P()),
+        out_specs=P(("high", "low", "near", "core"), None, None),
         check_vma=False,
     )

time: 61.2 us -> 59.7 us (0.975)
  waiting for transfers between devices: 17.3 us -> 13.2 us
  blocking collectives: 17 us -> 18.3 us
  starting transfers between devices: 22.1 us -> 23.3 us
    all_to_all x1, waiting for transfers between devices: 17.3 us -> 13.2 us  [body(): lax.all_to_all(rows.reshape(256, 4, LANES), ('high', 'low', 'near'), 0, 0...]
    all_to_all x1, blocking collectives: 17 us -> 18.3 us  [body(): owned = lax.all_to_all(spec, ('low', 'near', 'core'), 0, 0, tiled=True)]
    all_to_all x1, starting transfers between devices: 22.1 us -> 23.3 us  [body(): lax.all_to_all(rows.reshape(256, 4, LANES), ('high', 'low', 'near'), 0, 0...]
where the time goes in v3:
time: 59.7 us; the launch traced here: 59.5 us
  starting transfers between devices  23.3 us (39%)
  blocking collectives  18.3 us (31%)
  waiting for transfers between devices  13.2 us (22%)
  Pallas kernels  4.57 us (8%)
    all_to_all x1, starting transfers between devices, body(): lax.all_to_all(rows.reshape(256, 4, LANES), ('high', 'low', 'near'), 0, 0...  23.3 us
    all_to_all x1, blocking collectives, body(): owned = lax.all_to_all(spec, ('low', 'near', 'core'), 0, 0, tiled=True)  18.3 us
    all_to_all x1, waiting for transfers between devices, body(): lax.all_to_all(rows.reshape(256, 4, LANES), ('high', 'low', 'near'), 0, 0...  13.2 us
    pallas_call x1, Pallas kernels, whiten(): pl.pallas_call(whiten_kernel, out_shape=pltpu.VMEM((copies, LANES, LANES)...  1.82 us
    pallas_call x1, Pallas kernels, transform(): pl.pallas_call(transform_kernel, out_shape=jax.ShapeDtypeStruct((2, ROUND...  1.44 us
    pallas_call x1, Pallas kernels, cross(): pl.pallas_call(cross_kernel, out_shape=pltpu.VMEM((SLOTS, 8, LANES), jnp....  1.32 us
  transfers between devices with their start and end apart: 1, of which 1 were waited for; matrix products, arithmetic and copies ran while one was open for 0% of the time, Pallas kernels for 0%

profile of v3, /device:TPU:1, one launch (start us, length us, event | category | flops | bytes accessed | tf_op | source)
XLA Modules:
  0.0 59.5 jit_solution(9846193149834942332)
XLA Ops:
  0.0 0.0 copy-start.3
  0.0 0.0 copy-start.5
  0.0 1.8 %whiten.1 = bf16[8,128,128]{2,1,0:T(8,128)(2,1)} custom-call(f32[1,4,2,2048]{3,2,1,0:T(2,128)} %spectra_ref.1), custom_call_target="tpu_custom_call" | custom-call | tf_op jit(solution)/shard_map/whiten/pallas_call | solution.py:232
  1.8 0.0 copy-start
  1.8 23.3 %all-to-all-start = ((bf16[256,4,128]{2,1,0:T(4,128)(2,1)}), bf16[256,4,128]{2,1,0:T(4,128)(2,1)S(1)}, u32[]{:S(2)}, u32[]{:S(2)}) async-start(bf16[256,4,128]{2,1,0:T(4,128)(2,1)} %bitcast.1), calls=%async_computation | async-start | bytes 524288 | tf_op jit(solution)/shard_map/all_to_all | solution.py:274
  25.2 13.2 %all-to-all-done = bf16[256,4,128]{2,1,0:T(4,128)(2,1)S(1)} async-done(((bf16[256,4,128]{2,1,0:T(4,128)(2,1)}), bf16[256,4,128]{2,1,0:T(4,128)(2,1)S(1)}, u32[]{:S(2)}, u32[]{:S(2)}) %all-to-all-start) | async-done | bytes 262176 | tf_op jit(solution)/shard_map/all_to_all | solution.py:274
  38.4 0.0 copy-done.3
  38.4 0.0 copy-done.5
  38.4 0.0 copy-start.2
  38.4 0.0 copy-start.4
  38.4 1.3 %cross.1 = bf16[64,8,128]{2,1,0:T(8,128)(2,1)S(1)} custom-call(s32[4]{0:T(128)} %mask_ref.1, s32[1]{0:T(128)} %bitcast.home_ref, bf16[1024,128]{1,0:T(8,128)(2,1)S(1)} %bitcast.4, bf16[128,1024]{1,0:T(8,128)(2,1)S(1)} %copy-done.3, bf16[128,256]{1,0:T(8,128)(2,1)S(1)} %copy-done.5), custom_call_target="tpu_custom_call" | custom-call | tf_op jit(solution)/shard_map/cross/pallas_call | solution.py:245
  39.7 0.0 copy-start.1
  39.8 18.3 %all_to_all.10 = bf16[64,8,128]{2,1,0:T(8,128)(2,1)S(1)} all-to-all(bf16[64,8,128]{2,1,0:T(8,128)(2,1)S(1)} %cross.1), channel_id=1, replica_groups=mesh['high'=8,'low'=8,'near'=4,'core'=2] {'low','near','core'}, dimensions={0} | all-to-all | bytes 262144 | tf_op jit(solution)/shard_map/all_to_all | solution.py:279
  58.0 0.0 copy-done
  58.0 0.0 copy-done.2
  58.0 0.0 copy-done.4
  58.0 0.0 copy-done.1
  58.0 1.4 %transform.1 = f32[2,4,2400]{2,1,0:T(4,128)} custom-call(bf16[512,128]{1,0:T(8,128)(2,1)S(1)} %bitcast.5, bf16[384,1024]{1,0:T(8,128)(2,1)S(1)} %copy-done, f32[256,256]{1,0:T(8,128)S(1)} %copy-done.1, f32[256,256]{1,0:T(8,128)S(1)} %copy-done.2, bf16[4,80,256]{2,1,0:T(8,128)(2,1)S(1)} %copy-done.4), custom_call_target="tpu_custom_call" | custom-call | tf_op jit(solution)/shard_map/transform/pallas_call | solution.py:261
Async XLA Ops:
  0.0 38.4 %copy-start.3 = (bf16[128,1024]{1,0:T(8,128)(2,1)S(1)}, bf16[128,1024]{1,0:T(8,128)(2,1)}, u32[]{:S(2)}) copy-start(bf16[128,1024]{1,0:T(8,128)(2,1)} %constant.18.clone.own_table) | copy-start | bytes 786436
  0.0 38.4 %copy-start.5 = (bf16[128,256]{1,0:T(8,128)(2,1)S(1)}, bf16[128,256]{1,0:T(8,128)(2,1)}, u32[]{:S(2)}) copy-start(bf16[128,256]{1,0:T(8,128)(2,1)} %constant.19.clone.far_table) | copy-start | bytes 196612
  1.8 56.2 %copy-start = (bf16[384,1024]{1,0:T(8,128)(2,1)S(1)}, bf16[384,1024]{1,0:T(8,128)(2,1)}, u32[]{:S(2)}) copy-start(bf16[384,1024]{1,0:T(8,128)(2,1)} %constant.20.clone.first_ref) | copy-start | bytes 2359300
  1.8 36.6 %all-to-all-start = ((bf16[256,4,128]{2,1,0:T(4,128)(2,1)}), bf16[256,4,128]{2,1,0:T(4,128)(2,1)S(1)}, u32[]{:S(2)}, u32[]{:S(2)}) async-start(bf16[256,4,128]{2,1,0:T(4,128)(2,1)} %bitcast.1), calls=%async_computation | async-start | bytes 524288 | tf_op jit(solution)/shard_map/all_to_all | solution.py:274
  38.4 19.6 %copy-start.2 = (f32[256,256]{1,0:T(8,128)S(1)}, f32[256,256]{1,0:T(8,128)}, u32[]{:S(2)}) copy-start(f32[256,256]{1,0:T(8,128)} %constant.22.clone.sin_ref) | copy-start | bytes 786436
  38.4 19.6 %copy-start.4 = (bf16[4,80,256]{2,1,0:T(8,128)(2,1)S(1)}, bf16[4,80,256]{2,1,0:T(8,128)(2,1)}, u32[]{:S(2)}) copy-start(bf16[4,80,256]{2,1,0:T(8,128)(2,1)} %constant.23.clone.last_ref) | copy-start | bytes 491524
  39.7 18.3 %copy-start.1 = (f32[256,256]{1,0:T(8,128)S(1)}, f32[256,256]{1,0:T(8,128)}, u32[]{:S(2)}) copy-start(f32[256,256]{1,0:T(8,128)} %constant.21.clone.cos_ref) | copy-start | bytes 786436

commit v4 on v3

--- a/solution.py
+++ b/solution.py
@@ -123,8 +123,8 @@
         out_ref[copy] = turned
 
 
-def cross_kernel(mask_ref, home_ref, all_ref, own_table, far_table, out_ref, far_ref, left, right):
-    home = home_ref[0]
+def cross_kernel(mask_ref, all_ref, own_table, far_table, out_ref, far_ref, left, right):
+    home = lax.axis_index("high")
     own = all_ref[pl.ds(pl.multiple_of(home * 128, 128), 128), :]
     left[...] = jnp.dot(own, own_table[...], preferred_element_type=jnp.float32)
     for r in range(ROUNDS):
@@ -240,12 +240,12 @@
     )(spectra)
 
 
-def cross(partner_masks, home, gathered):
+def cross(partner_masks, gathered):
     own_table, far_table = selection_tables()
     return pl.pallas_call(
         cross_kernel,
         out_shape=pltpu.VMEM((SLOTS, 8, LANES), jnp.bfloat16),
-        in_specs=[spec_of(SMEM)] * 2 + [spec_of(VMEM)] * 3,
+        in_specs=[spec_of(SMEM)] + [spec_of(VMEM)] * 3,
         out_specs=spec_of(VMEM),
         scratch_shapes=[
             pltpu.VMEM((512, LANES), jnp.bfloat16),
@@ -254,7 +254,7 @@
         ],
         name="cross",
         interpret=INTERPRET,
-    )(partner_masks, home, *map(in_vmem, (gathered, own_table, far_table)))
+    )(pltpu.with_memory_space_constraint(partner_masks, SMEM), *map(in_vmem, (gathered, own_table, far_table)))
 
 
 def transform(spec_rows):
@@ -274,8 +274,7 @@
     gathered = lax.all_to_all(
         rows.reshape(256, 4, LANES), ("high", "low", "near"), 0, 0, tiled=True
     )
-    home = lax.axis_index("high").astype(jnp.int32).reshape(1)
-    spec = cross(partner_masks, home, gathered.reshape(1024, LANES))
+    spec = cross(partner_masks, gathered.reshape(1024, LANES))
     owned = lax.all_to_all(spec, ("low", "near", "core"), 0, 0, tiled=True)
     return transform(owned.reshape(SLOTS * 8, LANES))
 

time: 59.7 us -> 58.8 us (0.985)
  blocking collectives: 18.3 us -> 54.6 us
  starting transfers between devices: 23.3 us -> 0 us
  waiting for transfers between devices: 13.2 us -> 0 us
  Pallas kernels: 4.57 us -> 3.87 us
    all_to_all x0 -> x1, blocking collectives: none -> 36.5 us  [body(): lax.all_to_all(rows.reshape(256, 4, LANES), ('high', 'low', 'near'), 0, 0...]
    all_to_all x1 -> x0, starting transfers between devices: 23.3 us -> none  [body(): lax.all_to_all(rows.reshape(256, 4, LANES), ('high', 'low', 'near'), 0, 0...]
    all_to_all x1 -> x0, waiting for transfers between devices: 13.2 us -> none  [body(): lax.all_to_all(rows.reshape(256, 4, LANES), ('high', 'low', 'near'), 0, 0...]
    pallas_call x1, Pallas kernels: 1.82 us -> 1.11 us  [whiten(): pl.pallas_call(whiten_kernel, out_shape=pltpu.VMEM((copies, LANES, LANES)...]
  transfers between devices with their start and end apart: 1 -> 0, of which waited for: 1 -> 0; matrix products, arithmetic and copies ran while one was open for 0% -> 0% of each run, Pallas kernels for 0% -> 0%
where the time goes in v4:
time: 58.8 us; the launch traced here: 58.6 us
  blocking collectives  54.6 us (93%)
  Pallas kernels  3.87 us (7%)
    all_to_all x1, blocking collectives, body(): lax.all_to_all(rows.reshape(256, 4, LANES), ('high', 'low', 'near'), 0, 0...  36.5 us
    all_to_all x1, blocking collectives, body(): owned = lax.all_to_all(spec, ('low', 'near', 'core'), 0, 0, tiled=True)  18.1 us
    pallas_call x1, Pallas kernels, transform(): pl.pallas_call(transform_kernel, out_shape=jax.ShapeDtypeStruct((2, ROUND...  1.44 us
    pallas_call x1, Pallas kernels, cross(): pl.pallas_call(cross_kernel, out_shape=pltpu.VMEM((SLOTS, 8, LANES), jnp....  1.32 us

profile of v4, /device:TPU:1, one launch (start us, length us, event | category | flops | bytes accessed | tf_op | source)
XLA Modules:
  0.0 58.6 jit_solution(17198117637867333807)
XLA Ops:
  0.0 0.0 copy-start.3
  0.0 0.0 copy-start.5
  0.0 1.1 %whiten.1 = bf16[8,128,128]{2,1,0:T(8,128)(2,1)S(1)} custom-call(f32[1,4,2,2048]{3,2,1,0:T(2,128)} %spectra_ref.1), custom_call_target="tpu_custom_call" | custom-call | tf_op jit(solution)/shard_map/whiten/pallas_call | solution.py:232
  1.1 0.0 copy-start
  1.1 36.5 %all_to_all.10 = bf16[256,4,128]{2,1,0:T(4,128)(2,1)S(1)} all-to-all(bf16[256,4,128]{2,1,0:T(4,128)(2,1)S(1)} %bitcast.3), channel_id=1, replica_groups=mesh['high'=8,'low'=8,'near'=4,'core'=2] {'high','low','near'}, dimensions={0} | all-to-all | bytes 524288 | tf_op jit(solution)/shard_map/all_to_all | solution.py:274
  37.7 0.0 copy-done.3
  37.7 0.0 copy-done.5
  37.7 0.0 copy-start.2
  37.7 0.0 copy-start.4
  37.7 1.3 %cross.1 = bf16[64,8,128]{2,1,0:T(8,128)(2,1)S(1)} custom-call(s32[4]{0:T(128)} %mask_ref.1, bf16[1024,128]{1,0:T(8,128)(2,1)S(1)} %bitcast.4, bf16[128,1024]{1,0:T(8,128)(2,1)S(1)} %copy-done.3, bf16[128,256]{1,0:T(8,128)(2,1)S(1)} %copy-done.5), custom_call_target="tpu_custom_call" | custom-call | tf_op jit(solution)/shard_map/cross/pallas_call | solution.py:245
  39.0 0.0 copy-start.1
  39.0 18.1 %all_to_all.11 = bf16[64,8,128]{2,1,0:T(8,128)(2,1)S(1)} all-to-all(bf16[64,8,128]{2,1,0:T(8,128)(2,1)S(1)} %cross.1), channel_id=1, replica_groups=mesh['high'=8,'low'=8,'near'=4,'core'=2] {'low','near','core'}, dimensions={0} | all-to-all | bytes 262144 | tf_op jit(solution)/shard_map/all_to_all | solution.py:278
  57.1 0.0 copy-done
  57.1 0.0 copy-done.2
  57.1 0.0 copy-done.4
  57.1 0.0 copy-done.1
  57.1 1.4 %transform.1 = f32[2,4,2400]{2,1,0:T(4,128)} custom-call(bf16[512,128]{1,0:T(8,128)(2,1)S(1)} %bitcast.5, bf16[384,1024]{1,0:T(8,128)(2,1)S(1)} %copy-done, f32[256,256]{1,0:T(8,128)S(1)} %copy-done.2, f32[256,256]{1,0:T(8,128)S(1)} %copy-done.1, bf16[4,80,256]{2,1,0:T(8,128)(2,1)S(1)} %copy-done.4), custom_call_target="tpu_custom_call" | custom-call | tf_op jit(solution)/shard_map/transform/pallas_call | solution.py:261
Async XLA Ops:
  0.0 37.7 %copy-start.3 = (bf16[128,1024]{1,0:T(8,128)(2,1)S(1)}, bf16[128,1024]{1,0:T(8,128)(2,1)}, u32[]{:S(2)}) copy-start(bf16[128,1024]{1,0:T(8,128)(2,1)} %constant.12.clone.own_table) | copy-start | bytes 786436
  0.0 37.7 %copy-start.5 = (bf16[128,256]{1,0:T(8,128)(2,1)S(1)}, bf16[128,256]{1,0:T(8,128)(2,1)}, u32[]{:S(2)}) copy-start(bf16[128,256]{1,0:T(8,128)(2,1)} %constant.13.clone.far_table) | copy-start | bytes 196612
  1.1 56.0 %copy-start = (bf16[384,1024]{1,0:T(8,128)(2,1)S(1)}, bf16[384,1024]{1,0:T(8,128)(2,1)}, u32[]{:S(2)}) copy-start(bf16[384,1024]{1,0:T(8,128)(2,1)} %constant.14.clone.first_ref) | copy-start | bytes 2359300
  37.7 19.5 %copy-start.2 = (f32[256,256]{1,0:T(8,128)S(1)}, f32[256,256]{1,0:T(8,128)}, u32[]{:S(2)}) copy-start(f32[256,256]{1,0:T(8,128)} %constant.15.clone.cos_ref) | copy-start | bytes 786436
  37.7 19.5 %copy-start.4 = (bf16[4,80,256]{2,1,0:T(8,128)(2,1)S(1)}, bf16[4,80,256]{2,1,0:T(8,128)(2,1)}, u32[]{:S(2)}) copy-start(bf16[4,80,256]{2,1,0:T(8,128)(2,1)} %constant.17.clone.last_ref) | copy-start | bytes 491524
  39.0 18.1 %copy-start.1 = (f32[256,256]{1,0:T(8,128)S(1)}, f32[256,256]{1,0:T(8,128)}, u32[]{:S(2)}) copy-start(f32[256,256]{1,0:T(8,128)} %constant.16.clone.sin_ref) | copy-start | bytes 786436

commit v5 on v4

--- a/solution.py
+++ b/solution.py
@@ -24,7 +24,6 @@
 INTERPRET = False
 
 VMEM = pltpu.MemorySpace.VMEM
-SMEM = pltpu.MemorySpace.SMEM
 
 
 def split_bf16(table):
@@ -123,30 +122,29 @@
         out_ref[copy] = turned
 
 
-def cross_kernel(mask_ref, all_ref, own_table, far_table, out_ref, far_ref, left, right):
+def cross_kernel(mask_hbm, all_ref, own_table, far_table, out_ref, left, right, masks, sem):
+    fetch = pltpu.make_async_copy(mask_hbm, masks, sem)
+    fetch.start()
     home = lax.axis_index("high")
     own = all_ref[pl.ds(pl.multiple_of(home * 128, 128), 128), :]
     left[...] = jnp.dot(own, own_table[...], preferred_element_type=jnp.float32)
-    for r in range(ROUNDS):
-        mask = mask_ref[r]
-        high = (home ^ (mask >> 3)) & 7
-        for block in range(8):
-            other = (block ^ mask) & 7
-            start = pl.multiple_of(high * 128 + other * 16, 16)
-            far_ref[pl.ds(r * 128 + block * 16, 16), :] = all_ref[pl.ds(start, 16), :]
-    right[...] = jnp.dot(far_ref[...], far_table[...], preferred_element_type=jnp.float32)
+    right[...] = jnp.dot(all_ref[...], far_table[...], preferred_element_type=jnp.float32)
+    fetch.wait()
+    far = [((home ^ (masks[r] >> 3)) & 7) * 128 for r in range(ROUNDS)]
+    low = [masks[r] & 7 for r in range(ROUNDS)]
     sublane = lax.broadcasted_iota(jnp.int32, (8, LANES), 0)
     odd_round = sublane // 2 % 2 == 1
     lower = lax.broadcasted_iota(jnp.int32, (8, LANES), 1) < PAIR_LANES
 
     for block in range(8):
+        starts = [far[r] + (block ^ low[r]) * 16 for r in range(ROUNDS)]
         for i in range(STATIONS_HERE):
             straight = crossed = None
             for r in range(ROUNDS):
                 total = None
                 for step in range(2):
                     rows = pl.ds(block * 16 + step * 8, 8)
-                    far_rows = pl.ds(r * 128 + block * 16 + step * 8, 8)
+                    far_rows = pl.ds(pl.multiple_of(starts[r] + step * 8, 8), 8)
                     for part in range(2):
                         term = (
                             left[rows, pl.ds((part * 4 + i) * LANES, LANES)]
@@ -245,16 +243,17 @@
     return pl.pallas_call(
         cross_kernel,
         out_shape=pltpu.VMEM((SLOTS, 8, LANES), jnp.bfloat16),
-        in_specs=[spec_of(SMEM)] + [spec_of(VMEM)] * 3,
+        in_specs=[spec_of(pl.ANY)] + [spec_of(VMEM)] * 3,
         out_specs=spec_of(VMEM),
         scratch_shapes=[
-            pltpu.VMEM((512, LANES), jnp.bfloat16),
             pltpu.VMEM((LANES, 1024), jnp.float32),
-            pltpu.VMEM((512, 256), jnp.float32),
+            pltpu.VMEM((1024, 256), jnp.float32),
+            pltpu.SMEM((ROUNDS,), jnp.int32),
+            pltpu.SemaphoreType.DMA,
         ],
         name="cross",
         interpret=INTERPRET,
-    )(pltpu.with_memory_space_constraint(partner_masks, SMEM), *map(in_vmem, (gathered, own_table, far_table)))
+    )(partner_masks, *map(in_vmem, (gathered, own_table, far_table)))
 
 
 def transform(spec_rows):

time: 58.8 us -> 58.7 us (level)
  no operation moved by 1% of the time
where the time goes in v5:
time: 58.7 us; the launch traced here: 58.5 us
  blocking collectives  54.6 us (93%)
  Pallas kernels  3.76 us (6%)
    all_to_all x1, blocking collectives, body(): lax.all_to_all(rows.reshape(256, 4, LANES), ('high', 'low', 'near'), 0, 0...  36.5 us
    all_to_all x1, blocking collectives, body(): owned = lax.all_to_all(spec, ('low', 'near', 'core'), 0, 0, tiled=True)  18.1 us
    pallas_call x1, Pallas kernels, transform(): pl.pallas_call(transform_kernel, out_shape=jax.ShapeDtypeStruct((2, ROUND...  1.44 us
    pallas_call x1, Pallas kernels, cross(): pl.pallas_call(cross_kernel, out_shape=pltpu.VMEM((SLOTS, 8, LANES), jnp....  1.21 us

profile of v5, /device:TPU:1, one launch (start us, length us, event | category | flops | bytes accessed | tf_op | source)
XLA Modules:
  0.0 58.5 jit_solution(8027539324479275462)
XLA Ops:
  0.0 0.0 copy-start.3
  0.0 0.0 copy-start.5
  0.0 1.1 %whiten.1 = bf16[8,128,128]{2,1,0:T(8,128)(2,1)S(1)} custom-call(f32[1,4,2,2048]{3,2,1,0:T(2,128)} %spectra_ref.1), custom_call_target="tpu_custom_call" | custom-call | tf_op jit(solution)/shard_map/whiten/pallas_call | solution.py:230
  1.1 0.0 copy-start
  1.1 36.5 %all_to_all.10 = bf16[256,4,128]{2,1,0:T(4,128)(2,1)S(1)} all-to-all(bf16[256,4,128]{2,1,0:T(4,128)(2,1)S(1)} %bitcast.3), channel_id=1, replica_groups=mesh['high'=8,'low'=8,'near'=4,'core'=2] {'high','low','near'}, dimensions={0} | all-to-all | bytes 524288 | tf_op jit(solution)/shard_map/all_to_all | solution.py:273
  37.7 0.0 copy-done.3
  37.7 0.0 copy-done.5
  37.7 0.0 copy-start.2
  37.7 0.0 copy-start.4
  37.7 1.2 %cross.1 = bf16[64,8,128]{2,1,0:T(8,128)(2,1)S(1)} custom-call(s32[4]{0:T(128)} %mask_hbm.1, bf16[1024,128]{1,0:T(8,128)(2,1)S(1)} %bitcast.4, bf16[128,1024]{1,0:T(8,128)(2,1)S(1)} %copy-done.3, bf16[128,256]{1,0:T(8,128)(2,1)S(1)} %copy-done.5), custom_call_target="tpu_custom_call" | custom-call | tf_op jit(solution)/shard_map/cross/pallas_call | solution.py:243
  38.9 0.0 copy-start.1
  38.9 18.1 %all_to_all.11 = bf16[64,8,128]{2,1,0:T(8,128)(2,1)S(1)} all-to-all(bf16[64,8,128]{2,1,0:T(8,128)(2,1)S(1)} %cross.1), channel_id=1, replica_groups=mesh['high'=8,'low'=8,'near'=4,'core'=2] {'low','near','core'}, dimensions={0} | all-to-all | bytes 262144 | tf_op jit(solution)/shard_map/all_to_all | solution.py:277
  57.0 0.0 copy-done
  57.0 0.0 copy-done.2
  57.0 0.0 copy-done.4
  57.0 0.0 copy-done.1
  57.0 1.4 %transform.1 = f32[2,4,2400]{2,1,0:T(4,128)} custom-call(bf16[512,128]{1,0:T(8,128)(2,1)S(1)} %bitcast.5, bf16[384,1024]{1,0:T(8,128)(2,1)S(1)} %copy-done, f32[256,256]{1,0:T(8,128)S(1)} %copy-done.2, f32[256,256]{1,0:T(8,128)S(1)} %copy-done.1, bf16[4,80,256]{2,1,0:T(8,128)(2,1)S(1)} %copy-done.4), custom_call_target="tpu_custom_call" | custom-call | tf_op jit(solution)/shard_map/transform/pallas_call | solution.py:260
Async XLA Ops:
  0.0 37.7 %copy-start.3 = (bf16[128,1024]{1,0:T(8,128)(2,1)S(1)}, bf16[128,1024]{1,0:T(8,128)(2,1)}, u32[]{:S(2)}) copy-start(bf16[128,1024]{1,0:T(8,128)(2,1)} %constant.12.clone.own_table) | copy-start | bytes 786436
  0.0 37.7 %copy-start.5 = (bf16[128,256]{1,0:T(8,128)(2,1)S(1)}, bf16[128,256]{1,0:T(8,128)(2,1)}, u32[]{:S(2)}) copy-start(bf16[128,256]{1,0:T(8,128)(2,1)} %constant.13.clone.far_table) | copy-start | bytes 196612
  1.1 55.9 %copy-start = (bf16[384,1024]{1,0:T(8,128)(2,1)S(1)}, bf16[384,1024]{1,0:T(8,128)(2,1)}, u32[]{:S(2)}) copy-start(bf16[384,1024]{1,0:T(8,128)(2,1)} %constant.14.clone.first_ref) | copy-start | bytes 2359300
  37.7 19.3 %copy-start.2 = (f32[256,256]{1,0:T(8,128)S(1)}, f32[256,256]{1,0:T(8,128)}, u32[]{:S(2)}) copy-start(f32[256,256]{1,0:T(8,128)} %constant.15.clone.cos_ref) | copy-start | bytes 786436
  37.7 19.3 %copy-start.4 = (bf16[4,80,256]{2,1,0:T(8,128)(2,1)S(1)}, bf16[4,80,256]{2,1,0:T(8,128)(2,1)}, u32[]{:S(2)}) copy-start(bf16[4,80,256]{2,1,0:T(8,128)(2,1)} %constant.17.clone.last_ref) | copy-start | bytes 491524
  38.9 18.1 %copy-start.1 = (f32[256,256]{1,0:T(8,128)S(1)}, f32[256,256]{1,0:T(8,128)}, u32[]{:S(2)}) copy-start(f32[256,256]{1,0:T(8,128)} %constant.16.clone.sin_ref) | copy-start | bytes 786436

commit v6 on v4

--- a/solution.py
+++ b/solution.py
@@ -40,17 +40,16 @@
     half, out_coarse, low, out_part = lane // 64, lane // 4 % 16, lane // 2 % 2, lane % 2
     same_bin = coarse[:, None] == out_coarse[None, :]
     own = [
-        same_bin & (station == i)[:, None] & (part == c)[:, None]
-        for c in range(2)
+        same_bin & (station == i)[:, None] & (part[:, None] == half[None, :])
         for i in range(STATIONS_HERE)
     ]
     far_station = same_bin & (station[:, None] == (2 * half + low)[None, :])
-    match = (part[:, None] == out_part[None, :]) & far_station
-    cross = (part[:, None] != out_part[None, :]) & far_station
-    sign = np.where(out_part == 1, -1.0, 1.0)
+    match = np.where(out_part == 1, -1.0, 1.0) * (part[:, None] == out_part[None, :])
+    cross = 1.0 * (part[:, None] != out_part[None, :])
+    far = [far_station * np.where(half == side, match, cross) for side in range(2)]
     return (
         np.concatenate(own, axis=1).astype(jnp.bfloat16),
-        np.concatenate([match * sign, cross * 1.0], axis=1).astype(jnp.bfloat16),
+        np.concatenate(far, axis=1).astype(jnp.bfloat16),
     )
 
 
@@ -61,16 +60,14 @@
     base = (MAXLAG + shift) // LANES
     lane = np.arange(LANES)
     in_bit, coarse, pair, part = lane // 64, lane // 4 % 16, lane // 2 % 2, lane % 2
-    angle = 2 * np.pi * (coarse[:, None] * (f + shift)[None, :] % 64) / 64
-    cos, sin = np.cos(angle), np.sin(angle)
-    real = np.where(part[:, None] == 0, cos, -sin)
-    imag = np.where(part[:, None] == 0, sin, cos)
+    angle = 2 * np.pi * (coarse[:, None] * (f % 64 + shift)[None, :] % 64) / 64
+    angle = angle - np.where(f >= 64, np.pi / 2, 0.0)[None, :]
+    turned = np.where(part[:, None] == 0, np.cos(angle), -np.sin(angle))
     first = np.concatenate(
         [
-            np.where(((pair == p) & (in_bit == bit))[:, None], value, 0.0)
+            np.where(((pair == p) & (in_bit == bit))[:, None], turned, 0.0)
             for bit in range(2)
             for p in range(2)
-            for value in (real, imag)
         ],
         axis=1,
     )
@@ -80,6 +77,13 @@
     fine = 4 * (row // 8) + row % 2
     fine = np.repeat(np.stack([fine, fine + 2], axis=1), LANES, axis=1)
     twist = 2 * np.pi * (fine * np.tile(f + shift, 2)[None, :] % NFFT) / NFFT
+    cos, sin, early = np.cos(twist), np.sin(twist), np.tile(f < 64, 2)[None, :]
+    twists = [
+        np.where(early, cos, -sin),
+        np.where(early, -sin, cos),
+        np.where(early, sin, cos),
+        np.where(early, cos, sin),
+    ]
     out_row = np.arange(GROUP_ROWS)
     group, out_round = out_row // ROUNDS, out_row % ROUNDS
     in_row = np.arange(SHARES * 8)
@@ -88,17 +92,18 @@
     last = 2 * np.pi * (in_fine[None, :] * (group - base)[:, None] % 64) / 64
     keep = (out_round[:, None] == in_round[None, :]) & (group < GROUPS)[:, None]
     scale = 2.0 / math.sqrt(WINDOWS * COARSE * LANES)
-    cos_hi, cos_lo = split_bf16(np.where(keep, np.cos(last) * scale, 0.0))
-    sin_hi, sin_lo = split_bf16(np.where(keep, -np.sin(last) * scale, 0.0))
+    last = np.concatenate([np.cos(last), -np.sin(last)], axis=1) * scale
+    last_hi, last_lo = split_bf16(np.where(np.tile(keep, 2), last, 0.0))
     return (
         first,
-        np.cos(twist).astype(np.float32),
-        np.sin(twist).astype(np.float32),
-        np.stack([cos_hi, cos_lo, sin_hi, sin_lo]),
-    )
-
-
-def whiten_kernel(spectra_ref, out_ref, rows_ref):
+        np.stack(twists).astype(np.float32),
+        np.concatenate([last_hi, last_lo], axis=0),
+    )
+
+
+def whiten_kernel(spectra_ref, mask_ref, out_ref, mask_out, rows_ref):
+    for r in range(ROUNDS):
+        mask_out[r] = mask_ref[r]
     for station in range(STATIONS_HERE):
         for coarse in range(COARSE):
             rows_ref[pl.ds(coarse * 8 + station * 2, 2), :] = spectra_ref[
@@ -131,8 +136,7 @@
         mask = mask_ref[r]
         high = (home ^ (mask >> 3)) & 7
         for block in range(8):
-            other = (block ^ mask) & 7
-            start = pl.multiple_of(high * 128 + other * 16, 16)
+            start = pl.multiple_of(high * 128 + ((block ^ mask) & 7) * 16, 16)
             far_ref[pl.ds(r * 128 + block * 16, 16), :] = all_ref[pl.ds(start, 16), :]
     right[...] = jnp.dot(far_ref[...], far_table[...], preferred_element_type=jnp.float32)
     sublane = lax.broadcasted_iota(jnp.int32, (8, LANES), 0)
@@ -142,16 +146,16 @@
     for block in range(8):
         for i in range(STATIONS_HERE):
             straight = crossed = None
+            sides = []
+            for step in range(2):
+                side = left[pl.ds(block * 16 + step * 8, 8), pl.ds(i * LANES, LANES)]
+                sides.append((side, pltpu.roll(side, PAIR_LANES, 1)))
             for r in range(ROUNDS):
                 total = None
                 for step in range(2):
-                    rows = pl.ds(block * 16 + step * 8, 8)
                     far_rows = pl.ds(r * 128 + block * 16 + step * 8, 8)
                     for part in range(2):
-                        term = (
-                            left[rows, pl.ds((part * 4 + i) * LANES, LANES)]
-                            * right[far_rows, pl.ds(part * LANES, LANES)]
-                        )
+                        term = sides[step][part] * right[far_rows, pl.ds(part * LANES, LANES)]
                         total = term if total is None else total + term
                 total = total + pltpu.roll(total, 4, 0)
                 moved = pltpu.roll(total, 2, 0)
@@ -173,7 +177,7 @@
     return high, (value - high.astype(jnp.float32)).astype(jnp.bfloat16)
 
 
-def transform_kernel(spec_ref, first_ref, cos_ref, sin_ref, last_ref, out_ref, mid_ref):
+def transform_kernel(spec_ref, first_ref, twist_ref, last_ref, out_ref, mid_ref, high_ref, low_ref):
     both = spec_ref[...].astype(jnp.float32).reshape(SHARES, 2, 8, LANES)
     spec = both[:, 0] + both[:, 1]
     share = lax.broadcasted_iota(jnp.int32, spec.shape, 0)
@@ -188,29 +192,29 @@
         preferred_element_type=jnp.float32,
     )
     half = SHARES * 4
-    real, imag = [], []
-    for pair in range(2):
-        column_re, column_im = [], []
-        for bit in range(2):
-            parts_re, parts_im = [], []
+    for bit in range(2):
+        for start in range(0, half, 16):
+            sums = [[None, None], [None, None]]
             for side in range(2):
-                rows = pl.ds(side * half, half)
-                y_re = mid_ref[rows, pl.ds((bit * 4 + pair * 2) * LANES, LANES)]
-                y_im = mid_ref[rows, pl.ds((bit * 4 + pair * 2 + 1) * LANES, LANES)]
-                c = cos_ref[rows, pl.ds(bit * LANES, LANES)]
-                s = sin_ref[rows, pl.ds(bit * LANES, LANES)]
-                parts_re.append(y_re * c - y_im * s)
-                parts_im.append(y_re * s + y_im * c)
-            column_re.append(parts_re[0] + parts_re[1])
-            column_im.append(parts_im[0] + parts_im[1])
-        real.append(jnp.concatenate(column_re, axis=0))
-        imag.append(jnp.concatenate(column_im, axis=0))
-    total = None
-    for index, value in ((0, jnp.concatenate(real, axis=1)), (2, jnp.concatenate(imag, axis=1))):
-        high, low = split_value(value)
-        for table, operand in ((index, high), (index + 1, high), (index, low)):
-            term = jnp.dot(last_ref[table], operand, preferred_element_type=jnp.float32)
-            total = term if total is None else total + term
+                rows = pl.ds(side * half + start, 16)
+                twists = [twist_ref[t, rows, pl.ds(bit * LANES, LANES)] for t in range(4)]
+                for pair in range(2):
+                    value = mid_ref[rows, pl.ds((bit * 2 + pair) * LANES, LANES)]
+                    other = pltpu.roll(value, 64, 1)
+                    for part in range(2):
+                        term = value * twists[2 * part] + other * twists[2 * part + 1]
+                        known = sums[pair][part]
+                        sums[pair][part] = term if known is None else known + term
+            for pair in range(2):
+                for part in range(2):
+                    rows = pl.ds(part * 2 * half + bit * half + start, 16)
+                    columns = pl.ds(pair * LANES, LANES)
+                    high_ref[rows, columns], low_ref[rows, columns] = split_value(sums[pair][part])
+    double = jnp.dot(last_ref[...], high_ref[...], preferred_element_type=jnp.float32)
+    single = jnp.dot(
+        last_ref[pl.ds(0, GROUP_ROWS), :], low_ref[...], preferred_element_type=jnp.float32
+    )
+    total = double[:GROUP_ROWS] + double[GROUP_ROWS:] + single
     lags = out_ref.shape[2]
     for pair in range(2):
         for group in range(GROUPS):
@@ -228,16 +232,19 @@
     return pltpu.with_memory_space_constraint(jnp.asarray(array), VMEM)
 
 
-def whiten(spectra, copies):
+def whiten(spectra, partner_masks, copies):
     return pl.pallas_call(
         whiten_kernel,
-        out_shape=pltpu.VMEM((copies, LANES, LANES), jnp.bfloat16),
-        in_specs=[spec_of(VMEM)],
-        out_specs=spec_of(VMEM),
+        out_shape=(
+            pltpu.VMEM((copies, LANES, LANES), jnp.bfloat16),
+            pltpu.SMEM((ROUNDS,), jnp.int32),
+        ),
+        in_specs=[spec_of(VMEM), spec_of(SMEM)],
+        out_specs=(spec_of(VMEM), spec_of(SMEM)),
         scratch_shapes=[pltpu.VMEM((LANES, LANES), jnp.float32)],
         name="whiten",
         interpret=INTERPRET,
-    )(spectra)
+    )(spectra, partner_masks)
 
 
 def cross(partner_masks, gathered):
@@ -249,7 +256,7 @@
         out_specs=spec_of(VMEM),
         scratch_shapes=[
             pltpu.VMEM((512, LANES), jnp.bfloat16),
-            pltpu.VMEM((LANES, 1024), jnp.float32),
+            pltpu.VMEM((LANES, 512), jnp.float32),
             pltpu.VMEM((512, 256), jnp.float32),
         ],
         name="cross",
@@ -261,20 +268,24 @@
     return pl.pallas_call(
         transform_kernel,
         out_shape=jax.ShapeDtypeStruct((2, ROUNDS, 2 * MAXLAG), jnp.float32),
-        in_specs=[spec_of(VMEM)] * 5,
+        in_specs=[spec_of(VMEM)] * 4,
         out_specs=spec_of(VMEM),
-        scratch_shapes=[pltpu.VMEM((SHARES * 8, 1024), jnp.float32)],
+        scratch_shapes=[
+            pltpu.VMEM((SHARES * 8, 512), jnp.float32),
+            pltpu.VMEM((SHARES * 16, 256), jnp.bfloat16),
+            pltpu.VMEM((SHARES * 16, 256), jnp.bfloat16),
+        ],
         name="transform",
         interpret=INTERPRET,
     )(*map(in_vmem, (spec_rows, *transform_tables())))
 
 
 def body(spectra, partner_masks):
-    rows = whiten(spectra, lax.axis_size("high"))
+    rows, masks = whiten(spectra, partner_masks, lax.axis_size("high"))
     gathered = lax.all_to_all(
         rows.reshape(256, 4, LANES), ("high", "low", "near"), 0, 0, tiled=True
     )
-    spec = cross(partner_masks, gathered.reshape(1024, LANES))
+    spec = cross(masks, gathered.reshape(1024, LANES))
     owned = lax.all_to_all(spec, ("low", "near", "core"), 0, 0, tiled=True)
     return transform(owned.reshape(SLOTS * 8, LANES))
 

time: 58.8 us -> 60.4 us (1.027)
  local copies, waits for them, and re-layouts: 0.03 us -> 2.67 us
  Pallas kernels: 3.87 us -> 3.07 us
    unnamed x12 -> x10, local copies, waits for them, and re-layouts: 0.03 us -> 2.67 us
    pallas_call x1, Pallas kernels: 1.32 us -> 0.5 us  [cross(): pl.pallas_call(cross_kernel, out_shape=pltpu.VMEM((SLOTS, 8, LANES), jnp....]
where the time goes in v6:
time: 60.4 us; the launch traced here: 60.1 us
  blocking collectives  54.4 us (90%)
  Pallas kernels  3.07 us (5%)
  local copies, waits for them, and re-layouts  2.67 us (4%)
    all_to_all x1, blocking collectives, body(): lax.all_to_all(rows.reshape(256, 4, LANES), ('high', 'low', 'near'), 0, 0...  36.4 us
    all_to_all x1, blocking collectives, body(): owned = lax.all_to_all(spec, ('low', 'near', 'core'), 0, 0, tiled=True)  18 us
    unnamed x10, local copies, waits for them, and re-layouts  2.67 us
    pallas_call x1, Pallas kernels, transform(): pl.pallas_call(transform_kernel, out_shape=jax.ShapeDtypeStruct((2, ROUND...  1.41 us

profile of v6, /device:TPU:1, one launch (start us, length us, event | category | flops | bytes accessed | tf_op | source)
XLA Modules:
  0.0 60.1 jit_solution(5432654853418902128)
XLA Ops:
  0.0 0.0 copy-start
  0.0 1.2 %whiten.1 = (bf16[8,128,128]{2,1,0:T(8,128)(2,1)S(1)}, s32[4]{0:T(128)S(4)}) custom-call(f32[1,4,2,2048]{3,2,1,0:T(2,128)} %spectra_ref.1, s32[4]{0:T(128)} %mask_ref.1), custom_call_target="tpu_custom_call" | custom-call | tf_op jit(solution)/shard_map/whiten/pallas_call | solution.py:236
  1.2 36.4 %all_to_all.10 = bf16[256,4,128]{2,1,0:T(4,128)(2,1)S(1)} all-to-all(bf16[256,4,128]{2,1,0:T(4,128)(2,1)S(1)} %bitcast.5), channel_id=1, replica_groups=mesh['high'=8,'low'=8,'near'=4,'core'=2] {'high','low','near'}, dimensions={0} | all-to-all | bytes 524288 | tf_op jit(solution)/shard_map/all_to_all | solution.py:285
  37.6 0.0 copy-start.3
  37.6 0.9 %copy-done.3 = bf16[128,512]{1,0:T(8,128)(2,1)S(1)} copy-done((bf16[128,512]{1,0:T(8,128)(2,1)S(1)}, bf16[128,512]{1,0:T(8,128)(2,1)}, u32[]{:S(2)}) %copy-start.3) | copy-done | bytes 131096
  38.5 0.0 copy-start.4
  38.5 0.8 %copy-done.4 = bf16[128,256]{1,0:T(8,128)(2,1)S(1)} copy-done((bf16[128,256]{1,0:T(8,128)(2,1)S(1)}, bf16[128,256]{1,0:T(8,128)(2,1)}, u32[]{:S(2)}) %copy-start.4) | copy-done | bytes 65560
  39.3 0.0 copy-start.1
  39.3 0.5 cross.1
  39.8 18.0 %all_to_all.11 = bf16[64,8,128]{2,1,0:T(8,128)(2,1)S(1)} all-to-all(bf16[64,8,128]{2,1,0:T(8,128)(2,1)S(1)} %cross.1), channel_id=1, replica_groups=mesh['high'=8,'low'=8,'near'=4,'core'=2] {'low','near','core'}, dimensions={0} | all-to-all | bytes 262144 | tf_op jit(solution)/shard_map/all_to_all | solution.py:289
  57.8 0.0 copy-done
  57.8 0.0 copy-done.1
  57.8 0.0 copy-start.2
  57.8 0.9 %copy-done.2 = bf16[160,512]{1,0:T(8,128)(2,1)S(1)} copy-done((bf16[160,512]{1,0:T(8,128)(2,1)S(1)}, bf16[160,512]{1,0:T(8,128)(2,1)}, u32[]{:S(2)}) %copy-start.2) | copy-done | bytes 163864
  58.7 1.4 %transform.1 = f32[2,4,2400]{2,1,0:T(4,128)} custom-call(bf16[512,128]{1,0:T(8,128)(2,1)S(1)} %bitcast.4, bf16[384,512]{1,0:T(8,128)(2,1)S(1)} %copy-done.1, f32[4,256,256]{2,1,0:T(8,128)S(1)} %copy-done, bf16[160,512]{1,0:T(8,128)(2,1)S(1)} %copy-done.2), custom_call_target="tpu_custom_call" | custom-call | tf_op jit(solution)/shard_map/transform/pallas_call | solution.py:268
Async XLA Ops:
  0.0 57.8 %copy-start = (f32[4,256,256]{2,1,0:T(8,128)S(1)}, f32[4,256,256]{2,1,0:T(8,128)}, u32[]{:S(2)}) copy-start(f32[4,256,256]{2,1,0:T(8,128)} %constant.13.clone.twist_ref) | copy-start | bytes 3145732
  37.6 0.9 %copy-start.3 = (bf16[128,512]{1,0:T(8,128)(2,1)S(1)}, bf16[128,512]{1,0:T(8,128)(2,1)}, u32[]{:S(2)}) copy-start(bf16[128,512]{1,0:T(8,128)(2,1)} %constant.10.clone.own_table) | copy-start | bytes 393220
  38.5 0.8 %copy-start.4 = (bf16[128,256]{1,0:T(8,128)(2,1)S(1)}, bf16[128,256]{1,0:T(8,128)(2,1)}, u32[]{:S(2)}) copy-start(bf16[128,256]{1,0:T(8,128)(2,1)} %constant.11.clone.far_table) | copy-start | bytes 196612
  39.3 18.5 %copy-start.1 = (bf16[384,512]{1,0:T(8,128)(2,1)S(1)}, bf16[384,512]{1,0:T(8,128)(2,1)}, u32[]{:S(2)}) copy-start(bf16[384,512]{1,0:T(8,128)(2,1)} %constant.12.clone.first_ref) | copy-start | bytes 1179652
  57.8 0.9 %copy-start.2 = (bf16[160,512]{1,0:T(8,128)(2,1)S(1)}, bf16[160,512]{1,0:T(8,128)(2,1)}, u32[]{:S(2)}) copy-start(bf16[160,512]{1,0:T(8,128)(2,1)} %constant.14.clone.last_ref) | copy-start | bytes 491524

commit v7 on v4

--- a/solution.py
+++ b/solution.py
@@ -40,17 +40,16 @@
     half, out_coarse, low, out_part = lane // 64, lane // 4 % 16, lane // 2 % 2, lane % 2
     same_bin = coarse[:, None] == out_coarse[None, :]
     own = [
-        same_bin & (station == i)[:, None] & (part == c)[:, None]
-        for c in range(2)
+        same_bin & (station == i)[:, None] & (part[:, None] == half[None, :])
         for i in range(STATIONS_HERE)
     ]
     far_station = same_bin & (station[:, None] == (2 * half + low)[None, :])
-    match = (part[:, None] == out_part[None, :]) & far_station
-    cross = (part[:, None] != out_part[None, :]) & far_station
-    sign = np.where(out_part == 1, -1.0, 1.0)
+    match = np.where(out_part == 1, -1.0, 1.0) * (part[:, None] == out_part[None, :])
+    cross = 1.0 * (part[:, None] != out_part[None, :])
+    far = [far_station * np.where(half == side, match, cross) for side in range(2)]
     return (
         np.concatenate(own, axis=1).astype(jnp.bfloat16),
-        np.concatenate([match * sign, cross * 1.0], axis=1).astype(jnp.bfloat16),
+        np.concatenate(far, axis=1).astype(jnp.bfloat16),
     )
 
 
@@ -98,7 +97,13 @@
     )
 
 
-def whiten_kernel(spectra_ref, out_ref, rows_ref):
+def whiten_kernel(spectra_hbm, *refs):
+    inputs, (out_ref, *outputs), (spectra_ref, rows_ref, sems) = refs[:4], refs[4:9], refs[9:]
+    pairs = [(spectra_hbm, spectra_ref), *zip(inputs, outputs)]
+    copies = [pltpu.make_async_copy(*pair, sems.at[n]) for n, pair in enumerate(pairs)]
+    for copy in copies:
+        copy.start()
+    copies[0].wait()
     for station in range(STATIONS_HERE):
         for coarse in range(COARSE):
             rows_ref[pl.ds(coarse * 8 + station * 2, 2), :] = spectra_ref[
@@ -119,8 +124,10 @@
         for coarse in range(COARSE)
     ]
     turned = jnp.concatenate(white, axis=0).T.astype(jnp.bfloat16)
-    for copy in range(out_ref.shape[0]):
-        out_ref[copy] = turned
+    for index in range(out_ref.shape[0]):
+        out_ref[index] = turned
+    for copy in copies[1:]:
+        copy.wait()
 
 
 def cross_kernel(mask_ref, all_ref, own_table, far_table, out_ref, far_ref, left, right):
@@ -131,8 +138,7 @@
         mask = mask_ref[r]
         high = (home ^ (mask >> 3)) & 7
         for block in range(8):
-            other = (block ^ mask) & 7
-            start = pl.multiple_of(high * 128 + other * 16, 16)
+            start = pl.multiple_of(high * 128 + ((block ^ mask) & 7) * 16, 16)
             far_ref[pl.ds(r * 128 + block * 16, 16), :] = all_ref[pl.ds(start, 16), :]
     right[...] = jnp.dot(far_ref[...], far_table[...], preferred_element_type=jnp.float32)
     sublane = lax.broadcasted_iota(jnp.int32, (8, LANES), 0)
@@ -142,16 +148,16 @@
     for block in range(8):
         for i in range(STATIONS_HERE):
             straight = crossed = None
+            sides = []
+            for step in range(2):
+                side = left[pl.ds(block * 16 + step * 8, 8), pl.ds(i * LANES, LANES)]
+                sides.append((side, pltpu.roll(side, PAIR_LANES, 1)))
             for r in range(ROUNDS):
                 total = None
                 for step in range(2):
-                    rows = pl.ds(block * 16 + step * 8, 8)
                     far_rows = pl.ds(r * 128 + block * 16 + step * 8, 8)
                     for part in range(2):
-                        term = (
-                            left[rows, pl.ds((part * 4 + i) * LANES, LANES)]
-                            * right[far_rows, pl.ds(part * LANES, LANES)]
-                        )
+                        term = sides[step][part] * right[far_rows, pl.ds(part * LANES, LANES)]
                         total = term if total is None else total + term
                 total = total + pltpu.roll(total, 4, 0)
                 moved = pltpu.roll(total, 2, 0)
@@ -228,20 +234,28 @@
     return pltpu.with_memory_space_constraint(jnp.asarray(array), VMEM)
 
 
-def whiten(spectra, copies):
+def whiten(spectra, partner_masks, copies):
+    tables = [jnp.asarray(table) for table in (*selection_tables(), transform_tables()[-1])]
     return pl.pallas_call(
         whiten_kernel,
-        out_shape=pltpu.VMEM((copies, LANES, LANES), jnp.bfloat16),
-        in_specs=[spec_of(VMEM)],
-        out_specs=spec_of(VMEM),
-        scratch_shapes=[pltpu.VMEM((LANES, LANES), jnp.float32)],
+        out_shape=(
+            pltpu.VMEM((copies, LANES, LANES), jnp.bfloat16),
+            pltpu.SMEM((ROUNDS,), jnp.int32),
+            *[pltpu.VMEM(table.shape, table.dtype) for table in tables],
+        ),
+        in_specs=[spec_of(pl.ANY)] * 5,
+        out_specs=(spec_of(VMEM), spec_of(SMEM), *[spec_of(VMEM)] * 3),
+        scratch_shapes=[
+            pltpu.VMEM(spectra.shape, jnp.float32),
+            pltpu.VMEM((LANES, LANES), jnp.float32),
+            pltpu.SemaphoreType.DMA((5,)),
+        ],
         name="whiten",
         interpret=INTERPRET,
-    )(spectra)
-
-
-def cross(partner_masks, gathered):
-    own_table, far_table = selection_tables()
+    )(spectra, partner_masks, *tables)
+
+
+def cross(partner_masks, gathered, own_table, far_table):
     return pl.pallas_call(
         cross_kernel,
         out_shape=pltpu.VMEM((SLOTS, 8, LANES), jnp.bfloat16),
@@ -249,7 +263,7 @@
         out_specs=spec_of(VMEM),
         scratch_shapes=[
             pltpu.VMEM((512, LANES), jnp.bfloat16),
-            pltpu.VMEM((LANES, 1024), jnp.float32),
+            pltpu.VMEM((LANES, 512), jnp.float32),
             pltpu.VMEM((512, 256), jnp.float32),
         ],
         name="cross",
@@ -257,7 +271,7 @@
     )(pltpu.with_memory_space_constraint(partner_masks, SMEM), *map(in_vmem, (gathered, own_table, far_table)))
 
 
-def transform(spec_rows):
+def transform(spec_rows, last_table):
     return pl.pallas_call(
         transform_kernel,
         out_shape=jax.ShapeDtypeStruct((2, ROUNDS, 2 * MAXLAG), jnp.float32),
@@ -266,17 +280,19 @@
         scratch_shapes=[pltpu.VMEM((SHARES * 8, 1024), jnp.float32)],
         name="transform",
         interpret=INTERPRET,
-    )(*map(in_vmem, (spec_rows, *transform_tables())))
+    )(*map(in_vmem, (spec_rows, *transform_tables()[:-1], last_table)))
 
 
 def body(spectra, partner_masks):
-    rows = whiten(spectra, lax.axis_size("high"))
+    rows, masks, own_table, far_table, last_table = whiten(
+        spectra, partner_masks, lax.axis_size("high")
+    )
     gathered = lax.all_to_all(
         rows.reshape(256, 4, LANES), ("high", "low", "near"), 0, 0, tiled=True
     )
-    spec = cross(partner_masks, gathered.reshape(1024, LANES))
+    spec = cross(masks, gathered.reshape(1024, LANES), own_table, far_table)
     owned = lax.all_to_all(spec, ("low", "near", "core"), 0, 0, tiled=True)
-    return transform(owned.reshape(SLOTS * 8, LANES))
+    return transform(owned.reshape(SLOTS * 8, LANES), last_table)
 
 
 def solution(mesh):

time: 58.8 us -> 57.9 us (0.985)
  Pallas kernels: 3.87 us -> 3.07 us
    pallas_call x1, Pallas kernels: 1.32 us -> 0.5 us  [cross(): pl.pallas_call(cross_kernel, out_shape=pltpu.VMEM((SLOTS, 8, LANES), jnp....]
where the time goes in v7:
time: 57.9 us; the launch traced here: 57.7 us
  blocking collectives  54.6 us (94%)
  Pallas kernels  3.07 us (5%)
    all_to_all x1, blocking collectives, body(): lax.all_to_all(rows.reshape(256, 4, LANES), ('high', 'low', 'near'), 0, 0...  36.5 us
    all_to_all x1, blocking collectives, body(): owned = lax.all_to_all(spec, ('low', 'near', 'core'), 0, 0, tiled=True)  18.1 us
    pallas_call x1, Pallas kernels, transform(): pl.pallas_call(transform_kernel, out_shape=jax.ShapeDtypeStruct((2, ROUND...  1.44 us

profile of v7, /device:TPU:1, one launch (start us, length us, event | category | flops | bytes accessed | tf_op | source)
XLA Modules:
  0.0 57.7 jit_solution(6762487461439967955)
XLA Ops:
  0.0 1.1 %whiten.1 = (bf16[8,128,128]{2,1,0:T(8,128)(2,1)S(1)}, s32[4]{0:T(128)S(4)}, bf16[128,512]{1,0:T(8,128)(2,1)S(1)}, bf16[128,256]{1,0:T(8,128)(2,1)S(1)}, bf16[4,80,256]{2,1,0:T(8,128)(2,1)S(1)}) custom-call(f32[1,4,2,2048]{3,2,1,0:T(2,128)} %spectra_hbm.1, s32[4]{0:T(128)} %refs_0_.1, bf16[128,512]{1,0:T(8,128)(2,1)} %constant.12.clone.refs_1_, ...), custom_call_target="tpu_custom_call" | custom-call | tf_op jit(solution)/shard_map/whiten/pallas_call | solution.py:239
  1.1 0.0 copy-start
  1.1 36.5 %all_to_all.10 = bf16[256,4,128]{2,1,0:T(4,128)(2,1)S(1)} all-to-all(bf16[256,4,128]{2,1,0:T(4,128)(2,1)S(1)} %bitcast.5), channel_id=1, replica_groups=mesh['high'=8,'low'=8,'near'=4,'core'=2] {'high','low','near'}, dimensions={0} | all-to-all | bytes 524288 | tf_op jit(solution)/shard_map/all_to_all | solution.py:290
  37.7 0.0 copy-start.2
  37.7 0.5 cross.1
  38.2 0.0 copy-start.1
  38.2 18.1 %all_to_all.11 = bf16[64,8,128]{2,1,0:T(8,128)(2,1)S(1)} all-to-all(bf16[64,8,128]{2,1,0:T(8,128)(2,1)S(1)} %cross.1), channel_id=1, replica_groups=mesh['high'=8,'low'=8,'near'=4,'core'=2] {'low','near','core'}, dimensions={0} | all-to-all | bytes 262144 | tf_op jit(solution)/shard_map/all_to_all | solution.py:294
  56.3 0.0 copy-done
  56.3 0.0 copy-done.2
  56.3 0.0 copy-done.1
  56.3 1.4 %transform.1 = f32[2,4,2400]{2,1,0:T(4,128)} custom-call(bf16[512,128]{1,0:T(8,128)(2,1)S(1)} %bitcast.4, bf16[384,1024]{1,0:T(8,128)(2,1)S(1)} %copy-done, f32[256,256]{1,0:T(8,128)S(1)} %copy-done.2, f32[256,256]{1,0:T(8,128)S(1)} %copy-done.1, bf16[4,80,256]{2,1,0:T(8,128)(2,1)S(1)} %get-tuple-element.14.last_ref), custom_call_target="tpu_custom_call" | custom-call | tf_op jit(solution)/shard_map/transform/pallas_call | solution.py:275
Async XLA Ops:
  1.1 55.2 %copy-start = (bf16[384,1024]{1,0:T(8,128)(2,1)S(1)}, bf16[384,1024]{1,0:T(8,128)(2,1)}, u32[]{:S(2)}) copy-start(bf16[384,1024]{1,0:T(8,128)(2,1)} %constant.15.clone.first_ref) | copy-start | bytes 2359300
  37.7 18.6 %copy-start.2 = (f32[256,256]{1,0:T(8,128)S(1)}, f32[256,256]{1,0:T(8,128)}, u32[]{:S(2)}) copy-start(f32[256,256]{1,0:T(8,128)} %constant.16.clone.cos_ref) | copy-start | bytes 786436
  38.2 18.1 %copy-start.1 = (f32[256,256]{1,0:T(8,128)S(1)}, f32[256,256]{1,0:T(8,128)}, u32[]{:S(2)}) copy-start(f32[256,256]{1,0:T(8,128)} %constant.17.clone.sin_ref) | copy-start | bytes 786436

commit v8 on v7

--- a/solution.py
+++ b/solution.py
@@ -99,15 +99,16 @@
 
 def whiten_kernel(spectra_hbm, *refs):
     inputs, (out_ref, *outputs), (spectra_ref, rows_ref, sems) = refs[:4], refs[4:9], refs[9:]
-    pairs = [(spectra_hbm, spectra_ref), *zip(inputs, outputs)]
+    pairs = [(spectra_hbm.at[0, n], spectra_ref.at[n]) for n in range(STATIONS_HERE)]
+    pairs += zip(inputs, outputs)
     copies = [pltpu.make_async_copy(*pair, sems.at[n]) for n, pair in enumerate(pairs)]
     for copy in copies:
         copy.start()
-    copies[0].wait()
     for station in range(STATIONS_HERE):
+        copies[station].wait()
         for coarse in range(COARSE):
             rows_ref[pl.ds(coarse * 8 + station * 2, 2), :] = spectra_ref[
-                0, station, :, pl.ds(coarse * LANES, LANES)
+                station, :, pl.ds(coarse * LANES, LANES)
             ]
     even = lax.broadcasted_iota(jnp.int32, (8, LANES), 0) % 2 == 0
     power, total = [], None
@@ -126,7 +127,7 @@
     turned = jnp.concatenate(white, axis=0).T.astype(jnp.bfloat16)
     for index in range(out_ref.shape[0]):
         out_ref[index] = turned
-    for copy in copies[1:]:
+    for copy in copies[STATIONS_HERE:]:
         copy.wait()
 
 
@@ -179,7 +180,7 @@
     return high, (value - high.astype(jnp.float32)).astype(jnp.bfloat16)
 
 
-def transform_kernel(spec_ref, first_ref, cos_ref, sin_ref, last_ref, out_ref, mid_ref):
+def transform_kernel(spec_ref, first_ref, cos_ref, sin_ref, last_ref, out_hbm, mid_ref, out_ref, sems):
     both = spec_ref[...].astype(jnp.float32).reshape(SHARES, 2, 8, LANES)
     spec = both[:, 0] + both[:, 1]
     share = lax.broadcasted_iota(jnp.int32, spec.shape, 0)
@@ -218,12 +219,18 @@
             term = jnp.dot(last_ref[table], operand, preferred_element_type=jnp.float32)
             total = term if total is None else total + term
     lags = out_ref.shape[2]
+    copies = []
     for pair in range(2):
         for group in range(GROUPS):
             width = min(LANES, lags - group * LANES)
             out_ref[pair, :, pl.ds(group * LANES, width)] = total[
                 group * ROUNDS : (group + 1) * ROUNDS, pair * LANES : pair * LANES + width
             ]
+        copy = pltpu.make_async_copy(out_ref.at[pair], out_hbm.at[pair], sems.at[pair])
+        copy.start()
+        copies.append(copy)
+    for copy in copies:
+        copy.wait()
 
 
 def spec_of(space):
@@ -246,9 +253,9 @@
         in_specs=[spec_of(pl.ANY)] * 5,
         out_specs=(spec_of(VMEM), spec_of(SMEM), *[spec_of(VMEM)] * 3),
         scratch_shapes=[
-            pltpu.VMEM(spectra.shape, jnp.float32),
+            pltpu.VMEM(spectra.shape[1:], jnp.float32),
             pltpu.VMEM((LANES, LANES), jnp.float32),
-            pltpu.SemaphoreType.DMA((5,)),
+            pltpu.SemaphoreType.DMA((STATIONS_HERE + 4,)),
         ],
         name="whiten",
         interpret=INTERPRET,
@@ -276,8 +283,12 @@
         transform_kernel,
         out_shape=jax.ShapeDtypeStruct((2, ROUNDS, 2 * MAXLAG), jnp.float32),
         in_specs=[spec_of(VMEM)] * 5,
-        out_specs=spec_of(VMEM),
-        scratch_shapes=[pltpu.VMEM((SHARES * 8, 1024), jnp.float32)],
+        out_specs=spec_of(pl.ANY),
+        scratch_shapes=[
+            pltpu.VMEM((SHARES * 8, 1024), jnp.float32),
+            pltpu.VMEM((2, ROUNDS, 2 * MAXLAG), jnp.float32),
+            pltpu.SemaphoreType.DMA((2,)),
+        ],
         name="transform",
         interpret=INTERPRET,
     )(*map(in_vmem, (spec_rows, *transform_tables()[:-1], last_table)))

time: 57.9 us -> 58 us (level)
  no operation moved by 1% of the time
where the time goes in v8:
time: 58 us; the launch traced here: 57.8 us
  blocking collectives  54.6 us (94%)
  Pallas kernels  3.1 us (5%)
    all_to_all x1, blocking collectives, body(): lax.all_to_all(rows.reshape(256, 4, LANES), ('high', 'low', 'near'), 0, 0...  36.5 us
    all_to_all x1, blocking collectives, body(): owned = lax.all_to_all(spec, ('low', 'near', 'core'), 0, 0, tiled=True)  18.1 us
    pallas_call x1, Pallas kernels, transform(): pl.pallas_call(transform_kernel, out_shape=jax.ShapeDtypeStruct((2, ROUND...  1.45 us

profile of v8, /device:TPU:1, one launch (start us, length us, event | category | flops | bytes accessed | tf_op | source)
XLA Modules:
  0.0 57.8 jit_solution(13997563549689727839)
XLA Ops:
  0.0 1.1 %whiten.1 = (bf16[8,128,128]{2,1,0:T(8,128)(2,1)S(1)}, s32[4]{0:T(128)S(4)}, bf16[128,512]{1,0:T(8,128)(2,1)S(1)}, bf16[128,256]{1,0:T(8,128)(2,1)S(1)}, bf16[4,80,256]{2,1,0:T(8,128)(2,1)S(1)}) custom-call(f32[1,4,2,2048]{3,2,1,0:T(2,128)} %spectra_hbm.1, s32[4]{0:T(128)} %refs_0_.1, bf16[128,512]{1,0:T(8,128)(2,1)} %constant.12.clone.refs_1_, ...), custom_call_target="tpu_custom_call" | custom-call | tf_op jit(solution)/shard_map/whiten/pallas_call | solution.py:246
  1.2 0.0 copy-start
  1.2 36.5 %all_to_all.10 = bf16[256,4,128]{2,1,0:T(4,128)(2,1)S(1)} all-to-all(bf16[256,4,128]{2,1,0:T(4,128)(2,1)S(1)} %bitcast.5), channel_id=1, replica_groups=mesh['high'=8,'low'=8,'near'=4,'core'=2] {'high','low','near'}, dimensions={0} | all-to-all | bytes 524288 | tf_op jit(solution)/shard_map/all_to_all | solution.py:301
  37.7 0.0 copy-start.2
  37.7 0.5 cross.1
  38.2 0.0 copy-start.1
  38.2 18.1 %all_to_all.11 = bf16[64,8,128]{2,1,0:T(8,128)(2,1)S(1)} all-to-all(bf16[64,8,128]{2,1,0:T(8,128)(2,1)S(1)} %cross.1), channel_id=1, replica_groups=mesh['high'=8,'low'=8,'near'=4,'core'=2] {'low','near','core'}, dimensions={0} | all-to-all | bytes 262144 | tf_op jit(solution)/shard_map/all_to_all | solution.py:305
  56.3 0.0 copy-done
  56.3 0.0 copy-done.2
  56.3 0.0 copy-done.1
  56.3 1.5 %transform.1 = f32[2,4,2400]{2,1,0:T(4,128)} custom-call(bf16[512,128]{1,0:T(8,128)(2,1)S(1)} %bitcast.4, bf16[384,1024]{1,0:T(8,128)(2,1)S(1)} %copy-done, f32[256,256]{1,0:T(8,128)S(1)} %copy-done.2, f32[256,256]{1,0:T(8,128)S(1)} %copy-done.1, bf16[4,80,256]{2,1,0:T(8,128)(2,1)S(1)} %get-tuple-element.14.last_ref), custom_call_target="tpu_custom_call" | custom-call | tf_op jit(solution)/shard_map/transform/pallas_call | solution.py:282
Async XLA Ops:
  1.2 55.2 %copy-start = (bf16[384,1024]{1,0:T(8,128)(2,1)S(1)}, bf16[384,1024]{1,0:T(8,128)(2,1)}, u32[]{:S(2)}) copy-start(bf16[384,1024]{1,0:T(8,128)(2,1)} %constant.15.clone.first_ref) | copy-start | bytes 2359300
  37.7 18.6 %copy-start.2 = (f32[256,256]{1,0:T(8,128)S(1)}, f32[256,256]{1,0:T(8,128)}, u32[]{:S(2)}) copy-start(f32[256,256]{1,0:T(8,128)} %constant.16.clone.cos_ref) | copy-start | bytes 786436
  38.2 18.1 %copy-start.1 = (f32[256,256]{1,0:T(8,128)S(1)}, f32[256,256]{1,0:T(8,128)}, u32[]{:S(2)}) copy-start(f32[256,256]{1,0:T(8,128)} %constant.17.clone.sin_ref) | copy-start | bytes 786436

commit v9 on v8

--- a/solution.py
+++ b/solution.py
@@ -60,22 +60,25 @@
     base = (MAXLAG + shift) // LANES
     lane = np.arange(LANES)
     in_bit, coarse, pair, part = lane // 64, lane // 4 % 16, lane // 2 % 2, lane % 2
-    angle = 2 * np.pi * (coarse[:, None] * (f + shift)[None, :] % 64) / 64
-    cos, sin = np.cos(angle), np.sin(angle)
-    real = np.where(part[:, None] == 0, cos, -sin)
-    imag = np.where(part[:, None] == 0, sin, cos)
-    first = np.concatenate(
-        [
-            np.where(((pair == p) & (in_bit == bit))[:, None], value, 0.0)
-            for bit in range(2)
-            for p in range(2)
-            for value in (real, imag)
-        ],
-        axis=1,
-    )
-    first_hi, first_lo = split_bf16(first)
-    first = np.concatenate([first_hi, first_hi, first_lo], axis=0)
-    row = np.arange(SHARES * 8)
+    first = []
+    for side in range(2):
+        steps = (2 * coarse + side)[:, None] * (f + shift)[None, :] % LANES
+        cos, sin = np.cos(2 * np.pi * steps / LANES), np.sin(2 * np.pi * steps / LANES)
+        real = np.where(part[:, None] == 0, cos, -sin)
+        imag = np.where(part[:, None] == 0, sin, cos)
+        table = np.concatenate(
+            [
+                np.where(((pair == p) & (in_bit == bit))[:, None], value, 0.0)
+                for bit in range(2)
+                for p in range(2)
+                for value in (real, imag)
+            ],
+            axis=1,
+        )
+        high, low = split_bf16(table)
+        first += [high, high, low]
+    first = np.concatenate(first, axis=0)
+    row = np.arange(SHARES * 4)
     fine = 4 * (row // 8) + row % 2
     fine = np.repeat(np.stack([fine, fine + 2], axis=1), LANES, axis=1)
     twist = 2 * np.pi * (fine * np.tile(f + shift, 2)[None, :] % NFFT) / NFFT
@@ -87,18 +90,18 @@
     last = 2 * np.pi * (in_fine[None, :] * (group - base)[:, None] % 64) / 64
     keep = (out_round[:, None] == in_round[None, :]) & (group < GROUPS)[:, None]
     scale = 2.0 / math.sqrt(WINDOWS * COARSE * LANES)
-    cos_hi, cos_lo = split_bf16(np.where(keep, np.cos(last) * scale, 0.0))
-    sin_hi, sin_lo = split_bf16(np.where(keep, -np.sin(last) * scale, 0.0))
+    last = np.concatenate([np.cos(last), -np.sin(last)], axis=1) * scale
+    last_hi, last_lo = split_bf16(np.where(np.tile(keep, 2), last, 0.0))
     return (
         first,
         np.cos(twist).astype(np.float32),
         np.sin(twist).astype(np.float32),
-        np.stack([cos_hi, cos_lo, sin_hi, sin_lo]),
+        np.concatenate([last_hi, last_lo], axis=0),
     )
 
 
 def whiten_kernel(spectra_hbm, *refs):
-    inputs, (out_ref, *outputs), (spectra_ref, rows_ref, sems) = refs[:4], refs[4:9], refs[9:]
+    inputs, (out_ref, *outputs), (spectra_ref, rows_ref, sems) = refs[:6], refs[6:13], refs[13:]
     pairs = [(spectra_hbm.at[0, n], spectra_ref.at[n]) for n in range(STATIONS_HERE)]
     pairs += zip(inputs, outputs)
     copies = [pltpu.make_async_copy(*pair, sems.at[n]) for n, pair in enumerate(pairs)]
@@ -189,35 +192,34 @@
     zero_bin = (share == 0) & (row % 2 == 0) & (lane < 4)
     spec = jnp.where(zero_bin, 0.5 * spec, spec).reshape(SHARES * 8, LANES)
     high, low = split_value(spec)
+    half = SHARES * 4
     mid_ref[...] = jnp.dot(
-        jnp.concatenate([high, low, high], axis=1),
+        jnp.concatenate(
+            [high[:half], low[:half], high[:half], high[half:], low[half:], high[half:]], axis=1
+        ),
         first_ref[...],
         preferred_element_type=jnp.float32,
     )
-    half = SHARES * 4
     real, imag = [], []
     for pair in range(2):
         column_re, column_im = [], []
         for bit in range(2):
-            parts_re, parts_im = [], []
-            for side in range(2):
-                rows = pl.ds(side * half, half)
-                y_re = mid_ref[rows, pl.ds((bit * 4 + pair * 2) * LANES, LANES)]
-                y_im = mid_ref[rows, pl.ds((bit * 4 + pair * 2 + 1) * LANES, LANES)]
-                c = cos_ref[rows, pl.ds(bit * LANES, LANES)]
-                s = sin_ref[rows, pl.ds(bit * LANES, LANES)]
-                parts_re.append(y_re * c - y_im * s)
-                parts_im.append(y_re * s + y_im * c)
-            column_re.append(parts_re[0] + parts_re[1])
-            column_im.append(parts_im[0] + parts_im[1])
+            y_re = mid_ref[:, pl.ds((bit * 4 + pair * 2) * LANES, LANES)]
+            y_im = mid_ref[:, pl.ds((bit * 4 + pair * 2 + 1) * LANES, LANES)]
+            c = cos_ref[:, pl.ds(bit * LANES, LANES)]
+            s = sin_ref[:, pl.ds(bit * LANES, LANES)]
+            column_re.append(y_re * c - y_im * s)
+            column_im.append(y_re * s + y_im * c)
         real.append(jnp.concatenate(column_re, axis=0))
         imag.append(jnp.concatenate(column_im, axis=0))
-    total = None
-    for index, value in ((0, jnp.concatenate(real, axis=1)), (2, jnp.concatenate(imag, axis=1))):
-        high, low = split_value(value)
-        for table, operand in ((index, high), (index + 1, high), (index, low)):
-            term = jnp.dot(last_ref[table], operand, preferred_element_type=jnp.float32)
-            total = term if total is None else total + term
+    high, low = split_value(
+        jnp.concatenate([jnp.concatenate(real, axis=1), jnp.concatenate(imag, axis=1)], axis=0)
+    )
+    double = jnp.dot(last_ref[...], high, preferred_element_type=jnp.float32)
+    single = jnp.dot(
+        last_ref[pl.ds(0, GROUP_ROWS), :], low, preferred_element_type=jnp.float32
+    )
+    total = double[:GROUP_ROWS] + double[GROUP_ROWS:] + single
     lags = out_ref.shape[2]
     copies = []
     for pair in range(2):
@@ -242,7 +244,7 @@
 
 
 def whiten(spectra, partner_masks, copies):
-    tables = [jnp.asarray(table) for table in (*selection_tables(), transform_tables()[-1])]
+    tables = [jnp.asarray(table) for table in (*selection_tables(), *transform_tables()[1:])]
     return pl.pallas_call(
         whiten_kernel,
         out_shape=(
@@ -250,12 +252,12 @@
             pltpu.SMEM((ROUNDS,), jnp.int32),
             *[pltpu.VMEM(table.shape, table.dtype) for table in tables],
         ),
-        in_specs=[spec_of(pl.ANY)] * 5,
-        out_specs=(spec_of(VMEM), spec_of(SMEM), *[spec_of(VMEM)] * 3),
+        in_specs=[spec_of(pl.ANY)] * 7,
+        out_specs=(spec_of(VMEM), spec_of(SMEM), *[spec_of(VMEM)] * 5),
         scratch_shapes=[
             pltpu.VMEM(spectra.shape[1:], jnp.float32),
             pltpu.VMEM((LANES, LANES), jnp.float32),
-            pltpu.SemaphoreType.DMA((STATIONS_HERE + 4,)),
+            pltpu.SemaphoreType.DMA((STATIONS_HERE + 6,)),
         ],
         name="whiten",
         interpret=INTERPRET,
@@ -278,24 +280,24 @@
     )(pltpu.with_memory_space_constraint(partner_masks, SMEM), *map(in_vmem, (gathered, own_table, far_table)))
 
 
-def transform(spec_rows, last_table):
+def transform(spec_rows, *small_tables):
     return pl.pallas_call(
         transform_kernel,
         out_shape=jax.ShapeDtypeStruct((2, ROUNDS, 2 * MAXLAG), jnp.float32),
         in_specs=[spec_of(VMEM)] * 5,
         out_specs=spec_of(pl.ANY),
         scratch_shapes=[
-            pltpu.VMEM((SHARES * 8, 1024), jnp.float32),
+            pltpu.VMEM((SHARES * 4, 1024), jnp.float32),
             pltpu.VMEM((2, ROUNDS, 2 * MAXLAG), jnp.float32),
             pltpu.SemaphoreType.DMA((2,)),
         ],
         name="transform",
         interpret=INTERPRET,
-    )(*map(in_vmem, (spec_rows, *transform_tables()[:-1], last_table)))
+    )(*map(in_vmem, (spec_rows, transform_tables()[0], *small_tables)))
 
 
 def body(spectra, partner_masks):
-    rows, masks, own_table, far_table, last_table = whiten(
+    rows, masks, own_table, far_table, *small_tables = whiten(
         spectra, partner_masks, lax.axis_size("high")
     )
     gathered = lax.all_to_all(
@@ -303,7 +305,7 @@
     )
     spec = cross(masks, gathered.reshape(1024, LANES), own_table, far_table)
     owned = lax.all_to_all(spec, ("low", "near", "core"), 0, 0, tiled=True)
-    return transform(owned.reshape(SLOTS * 8, LANES), last_table)
+    return transform(owned.reshape(SLOTS * 8, LANES), *small_tables)
 
 
 def solution(mesh):

time: 58 us -> 57.7 us (level)
  no operation moved by 1% of the time
where the time goes in v9:
time: 57.7 us; the launch traced here: 57.5 us
  blocking collectives  54.4 us (94%)
  Pallas kernels  3.15 us (5%)
    all_to_all x1, blocking collectives, body(): lax.all_to_all(rows.reshape(256, 4, LANES), ('high', 'low', 'near'), 0, 0...  36.4 us
    all_to_all x1, blocking collectives, body(): owned = lax.all_to_all(spec, ('low', 'near', 'core'), 0, 0, tiled=True)  18 us
    pallas_call x1, Pallas kernels, whiten(): pl.pallas_call(whiten_kernel, out_shape=(pltpu.VMEM((copies, LANES, LANES...  1.41 us
    pallas_call x1, Pallas kernels, transform(): pl.pallas_call(transform_kernel, out_shape=jax.ShapeDtypeStruct((2, ROUND...  1.24 us

profile of v9, /device:TPU:1, one launch (start us, length us, event | category | flops | bytes accessed | tf_op | source)
XLA Modules:
  0.0 57.5 jit_solution(10637792413602965544)
XLA Ops:
  0.0 0.0 copy-start
  0.0 1.4 %whiten.1 = (bf16[8,128,128]{2,1,0:T(8,128)(2,1)S(1)}, s32[4]{0:T(128)S(4)}, bf16[128,512]{1,0:T(8,128)(2,1)S(1)}, bf16[128,256]{1,0:T(8,128)(2,1)S(1)}, f32[128...) custom-call(f32[1,4,2,2048]{3,2,1,0:T(2,128)} %spectra_hbm.1, s32[4]{0:T(128)} %refs_0_.1, ...), custom_call_target="tpu_custom_call" | custom-call | tf_op jit(solution)/shard_map/whiten/pallas_call | solution.py:248
  1.4 36.4 %all_to_all.10 = bf16[256,4,128]{2,1,0:T(4,128)(2,1)S(1)} all-to-all(bf16[256,4,128]{2,1,0:T(4,128)(2,1)S(1)} %bitcast.5), channel_id=1, replica_groups=mesh['high'=8,'low'=8,'near'=4,'core'=2] {'high','low','near'}, dimensions={0} | all-to-all | bytes 524288 | tf_op jit(solution)/shard_map/all_to_all | solution.py:303
  37.8 0.5 cross.1
  38.3 18.0 %all_to_all.11 = bf16[64,8,128]{2,1,0:T(8,128)(2,1)S(1)} all-to-all(bf16[64,8,128]{2,1,0:T(8,128)(2,1)S(1)} %cross.1), channel_id=1, replica_groups=mesh['high'=8,'low'=8,'near'=4,'core'=2] {'low','near','core'}, dimensions={0} | all-to-all | bytes 262144 | tf_op jit(solution)/shard_map/all_to_all | solution.py:307
  56.3 0.0 copy-done
  56.3 1.2 %transform.1 = f32[2,4,2400]{2,1,0:T(4,128)} custom-call(bf16[512,128]{1,0:T(8,128)(2,1)S(1)} %bitcast.4, bf16[768,1024]{1,0:T(8,128)(2,1)S(1)} %copy-done, f32[128,256]{1,0:T(8,128)S(1)} %get-tuple-element.16.cos_ref, f32[128,256]{1,0:T(8,128)S(1)} %get-tuple-element.17.sin_ref, bf16[160,512]{1,0:T(8,128)(2,1)S(1)} %get-tuple-element.18.last_ref), custom_call_target="tpu_custom_call" | custom-call | tf_op jit(solution)/shard_map/transform/pallas_call | solution.py:284
Async XLA Ops:
  0.0 56.3 %copy-start = (bf16[768,1024]{1,0:T(8,128)(2,1)S(1)}, bf16[768,1024]{1,0:T(8,128)(2,1)}, u32[]{:S(2)}) copy-start(bf16[768,1024]{1,0:T(8,128)(2,1)} %constant.17.clone.first_ref) | copy-start | bytes 4718596

commit v10 on v9

--- a/solution.py
+++ b/solution.py
@@ -77,7 +77,7 @@
         )
         high, low = split_bf16(table)
         first += [high, high, low]
-    first = np.concatenate(first, axis=0)
+    first = [np.concatenate(first[3 * side : 3 * side + 3], axis=0) for side in range(2)]
     row = np.arange(SHARES * 4)
     fine = 4 * (row // 8) + row % 2
     fine = np.repeat(np.stack([fine, fine + 2], axis=1), LANES, axis=1)
@@ -93,7 +93,7 @@
     last = np.concatenate([np.cos(last), -np.sin(last)], axis=1) * scale
     last_hi, last_lo = split_bf16(np.where(np.tile(keep, 2), last, 0.0))
     return (
-        first,
+        *first,
         np.cos(twist).astype(np.float32),
         np.sin(twist).astype(np.float32),
         np.concatenate([last_hi, last_lo], axis=0),
@@ -183,7 +183,7 @@
     return high, (value - high.astype(jnp.float32)).astype(jnp.bfloat16)
 
 
-def transform_kernel(spec_ref, first_ref, cos_ref, sin_ref, last_ref, out_hbm, mid_ref, out_ref, sems):
+def transform_kernel(spec_ref, first_ref, second_ref, cos_ref, sin_ref, last_ref, out_hbm, mid_ref, out_ref, sems):
     both = spec_ref[...].astype(jnp.float32).reshape(SHARES, 2, 8, LANES)
     spec = both[:, 0] + both[:, 1]
     share = lax.broadcasted_iota(jnp.int32, spec.shape, 0)
@@ -197,7 +197,7 @@
         jnp.concatenate(
             [high[:half], low[:half], high[:half], high[half:], low[half:], high[half:]], axis=1
         ),
-        first_ref[...],
+        jnp.concatenate([first_ref[...], second_ref[...]], axis=0),
         preferred_element_type=jnp.float32,
     )
     real, imag = [], []
@@ -244,7 +244,7 @@
 
 
 def whiten(spectra, partner_masks, copies):
-    tables = [jnp.asarray(table) for table in (*selection_tables(), *transform_tables()[1:])]
+    tables = [jnp.asarray(table) for table in (*selection_tables(), *transform_tables()[2:])]
     return pl.pallas_call(
         whiten_kernel,
         out_shape=(
@@ -284,7 +284,7 @@
     return pl.pallas_call(
         transform_kernel,
         out_shape=jax.ShapeDtypeStruct((2, ROUNDS, 2 * MAXLAG), jnp.float32),
-        in_specs=[spec_of(VMEM)] * 5,
+        in_specs=[spec_of(VMEM)] * 6,
         out_specs=spec_of(pl.ANY),
         scratch_shapes=[
             pltpu.VMEM((SHARES * 4, 1024), jnp.float32),
@@ -293,7 +293,7 @@
         ],
         name="transform",
         interpret=INTERPRET,
-    )(*map(in_vmem, (spec_rows, transform_tables()[0], *small_tables)))
+    )(*map(in_vmem, (spec_rows, *transform_tables()[:2], *small_tables)))
 
 
 def body(spectra, partner_masks):

time: 57.7 us -> 57.8 us (level)
  no operation moved by 1% of the time
where the time goes in v10:
time: 57.8 us; the launch traced here: 57.6 us
  blocking collectives  54.5 us (94%)
  Pallas kernels  3.1 us (5%)
    all_to_all x1, blocking collectives, body(): lax.all_to_all(rows.reshape(256, 4, LANES), ('high', 'low', 'near'), 0, 0...  36.5 us
    all_to_all x1, blocking collectives, body(): owned = lax.all_to_all(spec, ('low', 'near', 'core'), 0, 0, tiled=True)  18 us
    pallas_call x1, Pallas kernels, whiten(): pl.pallas_call(whiten_kernel, out_shape=(pltpu.VMEM((copies, LANES, LANES...  1.36 us
    pallas_call x1, Pallas kernels, transform(): pl.pallas_call(transform_kernel, out_shape=jax.ShapeDtypeStruct((2, ROUND...  1.24 us

profile of v10, /device:TPU:1, one launch (start us, length us, event | category | flops | bytes accessed | tf_op | source)
XLA Modules:
  0.0 57.6 jit_solution(17720844118522809509)
XLA Ops:
  0.0 0.0 copy-start.1
  0.0 1.4 %whiten.1 = (bf16[8,128,128]{2,1,0:T(8,128)(2,1)S(1)}, s32[4]{0:T(128)S(4)}, bf16[128,512]{1,0:T(8,128)(2,1)S(1)}, bf16[128,256]{1,0:T(8,128)(2,1)S(1)}, f32[128...) custom-call(f32[1,4,2,2048]{3,2,1,0:T(2,128)} %spectra_hbm.1, s32[4]{0:T(128)} %refs_0_.1, ...), custom_call_target="tpu_custom_call" | custom-call | tf_op jit(solution)/shard_map/whiten/pallas_call | solution.py:248
  1.4 0.0 copy-start
  1.4 36.5 %all_to_all.10 = bf16[256,4,128]{2,1,0:T(4,128)(2,1)S(1)} all-to-all(bf16[256,4,128]{2,1,0:T(4,128)(2,1)S(1)} %bitcast.5), channel_id=1, replica_groups=mesh['high'=8,'low'=8,'near'=4,'core'=2] {'high','low','near'}, dimensions={0} | all-to-all | bytes 524288 | tf_op jit(solution)/shard_map/all_to_all | solution.py:303
  37.9 0.5 cross.1
  38.4 18.0 %all_to_all.11 = bf16[64,8,128]{2,1,0:T(8,128)(2,1)S(1)} all-to-all(bf16[64,8,128]{2,1,0:T(8,128)(2,1)S(1)} %cross.1), channel_id=1, replica_groups=mesh['high'=8,'low'=8,'near'=4,'core'=2] {'low','near','core'}, dimensions={0} | all-to-all | bytes 262144 | tf_op jit(solution)/shard_map/all_to_all | solution.py:307
  56.4 0.0 copy-done.1
  56.4 0.0 copy-done
  56.4 1.2 %transform.1 = f32[2,4,2400]{2,1,0:T(4,128)} custom-call(bf16[512,128]{1,0:T(8,128)(2,1)S(1)} %bitcast.4, bf16[384,1024]{1,0:T(8,128)(2,1)S(1)} %copy-done.1, bf16[384,1024]{1,0:T(8,128)(2,1)S(1)} %copy-done, f32[128,256]{1,0:T(8,128)S(1)} %get-tuple-element.16.cos_ref, f32[128,256]{1,0:T(8,128)S(1)} %get-tuple-element.17.sin_ref, ...), custom_call_target="tpu_custom_call" | custom-call | tf_op jit(solution)/shard_map/transform/pallas_call | solution.py:284
Async XLA Ops:
  0.0 56.4 %copy-start.1 = (bf16[384,1024]{1,0:T(8,128)(2,1)S(1)}, bf16[384,1024]{1,0:T(8,128)(2,1)}, u32[]{:S(2)}) copy-start(bf16[384,1024]{1,0:T(8,128)(2,1)} %constant.19.clone.first_ref) | copy-start | bytes 2359300
  1.4 55.0 %copy-start = (bf16[384,1024]{1,0:T(8,128)(2,1)S(1)}, bf16[384,1024]{1,0:T(8,128)(2,1)}, u32[]{:S(2)}) copy-start(bf16[384,1024]{1,0:T(8,128)(2,1)} %constant.20.clone.second_ref) | copy-start | bytes 2359300

commit v11 on v10

--- a/solution.py
+++ b/solution.py
@@ -101,7 +101,7 @@
 
 
 def whiten_kernel(spectra_hbm, *refs):
-    inputs, (out_ref, *outputs), (spectra_ref, rows_ref, sems) = refs[:6], refs[6:13], refs[13:]
+    inputs, (out_ref, *outputs), (spectra_ref, rows_ref, sems) = refs[:3], refs[3:7], refs[7:]
     pairs = [(spectra_hbm.at[0, n], spectra_ref.at[n]) for n in range(STATIONS_HERE)]
     pairs += zip(inputs, outputs)
     copies = [pltpu.make_async_copy(*pair, sems.at[n]) for n, pair in enumerate(pairs)]
@@ -134,7 +134,13 @@
         copy.wait()
 
 
-def cross_kernel(mask_ref, all_ref, own_table, far_table, out_ref, far_ref, left, right):
+def cross_kernel(mask_ref, all_ref, own_table, far_table, *refs):
+    inputs, (out_ref, *outputs), (far_ref, left, right, sems) = refs[:3], refs[3:7], refs[7:]
+    copies = [
+        pltpu.make_async_copy(*pair, sems.at[n]) for n, pair in enumerate(zip(inputs, outputs))
+    ]
+    for copy in copies:
+        copy.start()
     home = lax.axis_index("high")
     own = all_ref[pl.ds(pl.multiple_of(home * 128, 128), 128), :]
     left[...] = jnp.dot(own, own_table[...], preferred_element_type=jnp.float32)
@@ -176,6 +182,8 @@
             out_ref[slot + 1] = jnp.where(
                 lower, pltpu.roll(first, PAIR_LANES, 1), second
             ).astype(jnp.bfloat16)
+    for copy in copies:
+        copy.wait()
 
 
 def split_value(value):
@@ -244,7 +252,7 @@
 
 
 def whiten(spectra, partner_masks, copies):
-    tables = [jnp.asarray(table) for table in (*selection_tables(), *transform_tables()[2:])]
+    tables = [jnp.asarray(table) for table in selection_tables()]
     return pl.pallas_call(
         whiten_kernel,
         out_shape=(
@@ -252,12 +260,12 @@
             pltpu.SMEM((ROUNDS,), jnp.int32),
             *[pltpu.VMEM(table.shape, table.dtype) for table in tables],
         ),
-        in_specs=[spec_of(pl.ANY)] * 7,
-        out_specs=(spec_of(VMEM), spec_of(SMEM), *[spec_of(VMEM)] * 5),
+        in_specs=[spec_of(pl.ANY)] * 4,
+        out_specs=(spec_of(VMEM), spec_of(SMEM), *[spec_of(VMEM)] * 2),
         scratch_shapes=[
             pltpu.VMEM(spectra.shape[1:], jnp.float32),
             pltpu.VMEM((LANES, LANES), jnp.float32),
-            pltpu.SemaphoreType.DMA((STATIONS_HERE + 6,)),
+            pltpu.SemaphoreType.DMA((STATIONS_HERE + 3,)),
         ],
         name="whiten",
         interpret=INTERPRET,
@@ -265,19 +273,24 @@
 
 
 def cross(partner_masks, gathered, own_table, far_table):
+    tables = [jnp.asarray(table) for table in transform_tables()[2:]]
     return pl.pallas_call(
         cross_kernel,
-        out_shape=pltpu.VMEM((SLOTS, 8, LANES), jnp.bfloat16),
-        in_specs=[spec_of(SMEM)] + [spec_of(VMEM)] * 3,
-        out_specs=spec_of(VMEM),
+        out_shape=(
+            pltpu.VMEM((SLOTS, 8, LANES), jnp.bfloat16),
+            *[pltpu.VMEM(table.shape, table.dtype) for table in tables],
+        ),
+        in_specs=[spec_of(SMEM)] + [spec_of(VMEM)] * 3 + [spec_of(pl.ANY)] * 3,
+        out_specs=(spec_of(VMEM),) * 4,
         scratch_shapes=[
             pltpu.VMEM((512, LANES), jnp.bfloat16),
             pltpu.VMEM((LANES, 512), jnp.float32),
             pltpu.VMEM((512, 256), jnp.float32),
+            pltpu.SemaphoreType.DMA((3,)),
         ],
         name="cross",
         interpret=INTERPRET,
-    )(pltpu.with_memory_space_constraint(partner_masks, SMEM), *map(in_vmem, (gathered, own_table, far_table)))
+    )(pltpu.with_memory_space_constraint(partner_masks, SMEM), *map(in_vmem, (gathered, own_table, far_table)), *tables)
 
 
 def transform(spec_rows, *small_tables):
@@ -297,13 +310,13 @@
 
 
 def body(spectra, partner_masks):
-    rows, masks, own_table, far_table, *small_tables = whiten(
+    rows, masks, own_table, far_table = whiten(
         spectra, partner_masks, lax.axis_size("high")
     )
     gathered = lax.all_to_all(
         rows.reshape(256, 4, LANES), ("high", "low", "near"), 0, 0, tiled=True
     )
-    spec = cross(masks, gathered.reshape(1024, LANES), own_table, far_table)
+    spec, *small_tables = cross(masks, gathered.reshape(1024, LANES), own_table, far_table)
     owned = lax.all_to_all(spec, ("low", "near", "core"), 0, 0, tiled=True)
     return transform(owned.reshape(SLOTS * 8, LANES), *small_tables)
 

time: 57.8 us -> 58.2 us (level)
    pallas_call x1, Pallas kernels: 0.5 us -> 1.17 us  [cross(): pl.pallas_call(cross_kernel, out_shape=(pltpu.VMEM((SLOTS, 8, LANES), jnp...]
where the time goes in v11:
time: 58.2 us; the launch traced here: 58 us
  blocking collectives  54.5 us (94%)
  Pallas kernels  3.47 us (6%)
    all_to_all x1, blocking collectives, body(): lax.all_to_all(rows.reshape(256, 4, LANES), ('high', 'low', 'near'), 0, 0...  36.5 us
    all_to_all x1, blocking collectives, body(): owned = lax.all_to_all(spec, ('low', 'near', 'core'), 0, 0, tiled=True)  18 us
    pallas_call x1, Pallas kernels, transform(): pl.pallas_call(transform_kernel, out_shape=jax.ShapeDtypeStruct((2, ROUND...  1.24 us
    pallas_call x1, Pallas kernels, cross(): pl.pallas_call(cross_kernel, out_shape=(pltpu.VMEM((SLOTS, 8, LANES), jnp...  1.17 us

profile of v11, /device:TPU:1, one launch (start us, length us, event | category | flops | bytes accessed | tf_op | source)
XLA Modules:
  0.0 58.0 jit_solution(9594769030802698387)
XLA Ops:
  0.0 1.1 %whiten.1 = (bf16[8,128,128]{2,1,0:T(8,128)(2,1)S(1)}, s32[4]{0:T(128)S(4)}, bf16[128,512]{1,0:T(8,128)(2,1)S(1)}, bf16[128,256]{1,0:T(8,128)(2,1)S(1)}) custom-call(f32[1,4,2,2048]{3,2,1,0:T(2,128)} %spectra_hbm.1, s32[4]{0:T(128)} %refs_0_.2, bf16[128,512]{1,0:T(8,128)(2,1)} %constant.14.clone.refs_1_, bf16[128,256]{1,0:T(8,128)(2,1)} %constant.15.clone.refs_2_), custom_call_target="tpu_custom_call" | custom-call | tf_op jit(solution)/shard_map/whiten/pallas_call | solution.py:256
  1.1 0.0 copy-start
  1.1 0.0 copy-start.1
  1.1 36.5 %all_to_all.10 = bf16[256,4,128]{2,1,0:T(4,128)(2,1)S(1)} all-to-all(bf16[256,4,128]{2,1,0:T(4,128)(2,1)S(1)} %bitcast.5), channel_id=1, replica_groups=mesh['high'=8,'low'=8,'near'=4,'core'=2] {'high','low','near'}, dimensions={0} | all-to-all | bytes 524288 | tf_op jit(solution)/shard_map/all_to_all | solution.py:316
  37.6 1.2 %cross.1 = (bf16[64,8,128]{2,1,0:T(8,128)(2,1)S(1)}, f32[128,256]{1,0:T(8,128)S(1)}, f32[128,256]{1,0:T(8,128)S(1)}, bf16[160,512]{1,0:T(8,128)(2,1)S(1)}) custom-call(s32[4]{0:T(128)S(4)} %get-tuple-element.13.mask_ref, bf16[1024,128]{1,0:T(8,128)(2,1)S(1)} %bitcast.3, bf16[128,512]{1,0:T(8,128)(2,1)S(1)} %get-tuple-element.15.own_table, ...), custom_call_target="tpu_custom_call" | custom-call | tf_op jit(solution)/shard_map/cross/pallas_call | solution.py:277
  38.8 18.0 %all_to_all.11 = bf16[64,8,128]{2,1,0:T(8,128)(2,1)S(1)} all-to-all(bf16[64,8,128]{2,1,0:T(8,128)(2,1)S(1)} %get-tuple-element.17), channel_id=1, replica_groups=mesh['high'=8,'low'=8,'near'=4,'core'=2] {'low','near','core'}, dimensions={0} | all-to-all | bytes 262144 | tf_op jit(solution)/shard_map/all_to_all | solution.py:320
  56.8 0.0 copy-done
  56.8 0.0 copy-done.1
  56.8 1.2 %transform.1 = f32[2,4,2400]{2,1,0:T(4,128)} custom-call(bf16[512,128]{1,0:T(8,128)(2,1)S(1)} %bitcast.4, bf16[384,1024]{1,0:T(8,128)(2,1)S(1)} %copy-done.1, bf16[384,1024]{1,0:T(8,128)(2,1)S(1)} %copy-done, f32[128,256]{1,0:T(8,128)S(1)} %get-tuple-element.18.cos_ref, f32[128,256]{1,0:T(8,128)S(1)} %get-tuple-element.19.sin_ref, ...), custom_call_target="tpu_custom_call" | custom-call | tf_op jit(solution)/shard_map/transform/pallas_call | solution.py:297
Async XLA Ops:
  1.1 55.7 %copy-start = (bf16[384,1024]{1,0:T(8,128)(2,1)S(1)}, bf16[384,1024]{1,0:T(8,128)(2,1)}, u32[]{:S(2)}) copy-start(bf16[384,1024]{1,0:T(8,128)(2,1)} %constant.20.clone.second_ref) | copy-start | bytes 2359300
  1.1 55.7 %copy-start.1 = (bf16[384,1024]{1,0:T(8,128)(2,1)S(1)}, bf16[384,1024]{1,0:T(8,128)(2,1)}, u32[]{:S(2)}) copy-start(bf16[384,1024]{1,0:T(8,128)(2,1)} %constant.19.clone.first_ref) | copy-start | bytes 2359300

commit v12 on v10

--- a/solution.py
+++ b/solution.py
@@ -105,8 +105,8 @@
     pairs = [(spectra_hbm.at[0, n], spectra_ref.at[n]) for n in range(STATIONS_HERE)]
     pairs += zip(inputs, outputs)
     copies = [pltpu.make_async_copy(*pair, sems.at[n]) for n, pair in enumerate(pairs)]
-    for copy in copies:
-        copy.start()
+    for n, copy in enumerate(copies):
+        copy.start(priority=int(n >= STATIONS_HERE))
     for station in range(STATIONS_HERE):
         copies[station].wait()
         for coarse in range(COARSE):

time: 57.8 us -> 57.8 us (level)
  no operation moved by 1% of the time
where the time goes in v12:
time: 57.8 us; the launch traced here: 57.6 us
  blocking collectives  54.5 us (94%)
  Pallas kernels  3.1 us (5%)
    all_to_all x1, blocking collectives, body(): lax.all_to_all(rows.reshape(256, 4, LANES), ('high', 'low', 'near'), 0, 0...  36.5 us
    all_to_all x1, blocking collectives, body(): owned = lax.all_to_all(spec, ('low', 'near', 'core'), 0, 0, tiled=True)  18 us
    pallas_call x1, Pallas kernels, whiten(): pl.pallas_call(whiten_kernel, out_shape=(pltpu.VMEM((copies, LANES, LANES...  1.36 us
    pallas_call x1, Pallas kernels, transform(): pl.pallas_call(transform_kernel, out_shape=jax.ShapeDtypeStruct((2, ROUND...  1.24 us

profile of v12, /device:TPU:1, one launch (start us, length us, event | category | flops | bytes accessed | tf_op | source)
XLA Modules:
  0.0 57.6 jit_solution(2594511920116536543)
XLA Ops:
  0.0 0.0 copy-start.1
  0.0 1.4 %whiten.1 = (bf16[8,128,128]{2,1,0:T(8,128)(2,1)S(1)}, s32[4]{0:T(128)S(4)}, bf16[128,512]{1,0:T(8,128)(2,1)S(1)}, bf16[128,256]{1,0:T(8,128)(2,1)S(1)}, f32[128...) custom-call(f32[1,4,2,2048]{3,2,1,0:T(2,128)} %spectra_hbm.1, s32[4]{0:T(128)} %refs_0_.1, ...), custom_call_target="tpu_custom_call" | custom-call | tf_op jit(solution)/shard_map/whiten/pallas_call | solution.py:248
  1.4 0.0 copy-start
  1.4 36.5 %all_to_all.10 = bf16[256,4,128]{2,1,0:T(4,128)(2,1)S(1)} all-to-all(bf16[256,4,128]{2,1,0:T(4,128)(2,1)S(1)} %bitcast.5), channel_id=1, replica_groups=mesh['high'=8,'low'=8,'near'=4,'core'=2] {'high','low','near'}, dimensions={0} | all-to-all | bytes 524288 | tf_op jit(solution)/shard_map/all_to_all | solution.py:303
  37.9 0.5 cross.1
  38.4 18.0 %all_to_all.11 = bf16[64,8,128]{2,1,0:T(8,128)(2,1)S(1)} all-to-all(bf16[64,8,128]{2,1,0:T(8,128)(2,1)S(1)} %cross.1), channel_id=1, replica_groups=mesh['high'=8,'low'=8,'near'=4,'core'=2] {'low','near','core'}, dimensions={0} | all-to-all | bytes 262144 | tf_op jit(solution)/shard_map/all_to_all | solution.py:307
  56.4 0.0 copy-done.1
  56.4 0.0 copy-done
  56.4 1.2 %transform.1 = f32[2,4,2400]{2,1,0:T(4,128)} custom-call(bf16[512,128]{1,0:T(8,128)(2,1)S(1)} %bitcast.4, bf16[384,1024]{1,0:T(8,128)(2,1)S(1)} %copy-done.1, bf16[384,1024]{1,0:T(8,128)(2,1)S(1)} %copy-done, f32[128,256]{1,0:T(8,128)S(1)} %get-tuple-element.16.cos_ref, f32[128,256]{1,0:T(8,128)S(1)} %get-tuple-element.17.sin_ref, ...), custom_call_target="tpu_custom_call" | custom-call | tf_op jit(solution)/shard_map/transform/pallas_call | solution.py:284
Async XLA Ops:
  0.0 56.4 %copy-start.1 = (bf16[384,1024]{1,0:T(8,128)(2,1)S(1)}, bf16[384,1024]{1,0:T(8,128)(2,1)}, u32[]{:S(2)}) copy-start(bf16[384,1024]{1,0:T(8,128)(2,1)} %constant.19.clone.first_ref) | copy-start | bytes 2359300
  1.4 55.0 %copy-start = (bf16[384,1024]{1,0:T(8,128)(2,1)S(1)}, bf16[384,1024]{1,0:T(8,128)(2,1)}, u32[]{:S(2)}) copy-start(bf16[384,1024]{1,0:T(8,128)(2,1)} %constant.20.clone.second_ref) | copy-start | bytes 2359300
